TPU v7x, 32 devices: a whole 2x2x4 slice. The times are simulated.
32 devices in a mesh: parts: 2 (over x), img: 16 (over z, y, core).
Axes of the slice: x: 2, y: 2, z: 4, core: 2. Of those that a mesh axis runs over, the one named last changes fastest.
Arguments:
- images: bfloat16 [2048, 16384], P(('parts', 'img')), parts along dimension 0, may hold values from -28 to 28
- groups: int32 [2048], P(('parts', 'img')), parts along dimension 0, may hold values from 0 to 7
- shifts: int32 [18, 2], P('parts'), parts along dimension 0, may hold values from -3 to 3
- volume: bfloat16 [32768, 256], P(('parts', 'img')), parts along dimension 0, may hold values from -6 to 6
- owner: int32 [8192, 1], P('parts'), parts along dimension 0, may hold values from 0 to 15; in each aligned block of 4096 rows (0 to 4095, 4096 to 8191, ...) at most 384 rows name the same one
- local: int32 [8192], P('parts'), parts along dimension 0, may hold values from 0 to 1023
- table_id: int32 [8192], P('parts'), parts along dimension 0, may hold values from 0 to 7
- interp: bfloat16 [8, 128, 128], replicated, may hold values from -0.5 to 0.5
- ctf: float32 [16, 8192], P('parts'), parts along dimension 0, may hold values from 0.2 to 1
Outputs:
- new_map: float32 [32768, 256], P(('parts', 'img')), parts along dimension 0
- evidence: float32 [2048], P(('parts', 'img')), parts along dimension 0
There are 2 independent parts, one for each index of `parts`. A program takes and returns all parts, laid end to end along the dimension named above; an argument that names none is the same for every part. Nothing has to cross between parts.
Inputs may be any that keep to these rules, and one draw needn't show every extreme that they name: `owner`: no slab is named by more than 384 slice blocks, a bound that some block reaches.
All inputs are finite; a program needn't handle non-finite values.
Results may differ from a plain program's by a relative error of at most 0.012.
The roundings to bfloat16 on the way count: a program that leaves them out, or rounds other values in their place, can miss the bound.
Values may be sent and summed in bfloat16 or wider, within the bound.
A program may use at most 128 MiB of HBM per device.

v0:
```python
import math

import jax
import jax.numpy as jnp
from jax import lax
from jax.sharding import PartitionSpec as P

BW = 128
KB = 64
R = 64


exact_mode = lax.Precision.HIGHEST


def phases(shifts):
    freq_x = (jnp.arange(BW) - BW // 2).astype(jnp.float32)
    freq_y = jnp.arange(KB).astype(jnp.float32)
    shift_x = shifts[:, 0].astype(jnp.float32)
    shift_y = shifts[:, 1].astype(jnp.float32)
    angles = (
        2.0
        * math.pi
        / BW
        * (
            shift_x[:, None, None] * freq_x[None, None, :]
            + shift_y[:, None, None] * freq_y[None, :, None]
        )
    )
    return (jnp.cos(angles), jnp.sin(angles))


def pick_table(blocks_in, table_ids, interp, adjoint):
    tables = interp.astype(jnp.float32)
    if adjoint:
        expanded = jnp.einsum("ncj,tjv->ntcv", blocks_in, tables, precision=exact_mode)
    else:
        expanded = jnp.einsum("ncv,tjv->ntcj", blocks_in, tables, precision=exact_mode)
    one_hot = (table_ids[:, None] == jnp.arange(interp.shape[0])[None, :]).astype(jnp.float32)
    return jnp.sum(expanded * one_hot[:, :, None, None], axis=1)


def score_images(image_rows, group_ids, slices, shifts, ctf):
    refs = slices.shape[0]
    count = image_rows.shape[0]
    cosine, sine_values = phases(shifts)
    slice_values = slices.astype(jnp.float32)
    powers = (slice_values[:, :, 0] ** 2 + slice_values[:, :, 1] ** 2).reshape(refs, KB * BW)
    norm_terms = jnp.dot(ctf * ctf, powers.T, precision=exact_mode)
    one_hot = (group_ids[:, None] == jnp.arange(ctf.shape[0])[None, :]).astype(jnp.float32)
    image_ctf = jnp.dot(one_hot, ctf, precision=exact_mode).reshape(count, KB, 1, BW)
    weighted = (
        (image_rows.astype(jnp.float32).reshape(count, KB, 2, BW) * image_ctf)
        .astype(jnp.bfloat16)
        .reshape(count, KB * 2 * BW)
    )
    image_norms = jnp.dot(one_hot, norm_terms, precision=exact_mode)
    scale_factor = 1.0 / math.sqrt(KB * BW)
    score_list = []
    for number in range(cosine.shape[0]):
        real_part = (
            slice_values[:, :, 0] * cosine[number] - slice_values[:, :, 1] * sine_values[number]
        )
        imag_part = (
            slice_values[:, :, 0] * sine_values[number] + slice_values[:, :, 1] * cosine[number]
        )
        rotated = (
            jnp.stack([real_part, imag_part], axis=2)
            .astype(jnp.bfloat16)
            .reshape(refs, KB * 2 * BW)
        )
        intersection = lax.dot_general(
            weighted, rotated, (((1,), (1,)), ((), ())), preferred_element_type=jnp.float32
        )
        score_list.append((intersection - 0.5 * image_norms) * scale_factor)
    scores = jnp.stack(score_list, axis=1)
    maximum = jnp.max(scores, axis=(1, 2))
    exponent = jnp.exp(scores - maximum[:, None, None])
    summed = jnp.sum(exponent, axis=(1, 2))
    evidence = maximum + jnp.log(summed)
    weights = (exponent / summed[:, None, None]).astype(jnp.bfloat16)
    accumulated = jnp.zeros((refs, KB, 2, BW), jnp.float32)
    for number in range(cosine.shape[0]):
        partial_sum = lax.dot_general(
            weights[:, number, :],
            weighted,
            (((0,), (0,)), ((), ())),
            preferred_element_type=jnp.float32,
        ).reshape(refs, KB, 2, BW)
        back_real = (
            partial_sum[:, :, 0] * cosine[number] + partial_sum[:, :, 1] * sine_values[number]
        )
        back_imag = (
            partial_sum[:, :, 1] * cosine[number] - partial_sum[:, :, 0] * sine_values[number]
        )
        accumulated = accumulated + jnp.stack([back_real, back_imag], axis=2)
    return (accumulated, evidence)


def per_device(images, groups, shifts, volume, owner, local, table_id, interp, ctf):
    devices = lax.axis_size("img")
    myself = lax.axis_index("img")
    block_count = R * KB
    capacity = max(2, 3 * block_count // (2 * devices))
    owners = owner[:, 0]
    member = (owners[:, None] == jnp.arange(devices, dtype=jnp.int32)[None, :]).astype(jnp.int32)
    position = jnp.sum(jnp.cumsum(member, axis=0) * member, axis=1) - 1
    target = owners * capacity + position
    owned = owners == myself
    slot_source = (
        jnp.full((capacity,), block_count, jnp.int32)
        .at[jnp.where(owned, position, capacity)]
        .set(jnp.arange(block_count, dtype=jnp.int32), mode="drop")
    )
    local_padded = jnp.concatenate([local, jnp.zeros((1,), jnp.int32)])
    table_padded = jnp.concatenate([table_id, jnp.zeros((1,), jnp.int32)])
    slot_local = local_padded[slot_source]
    slot_table = table_padded[slot_source]
    volume_rows = volume[slot_local].astype(jnp.float32).reshape(capacity, 2, BW)
    own_slices = (
        pick_table(volume_rows, slot_table, interp, False)
        .astype(jnp.bfloat16)
        .reshape(capacity, 2 * BW)
    )
    gathered = lax.all_gather(own_slices, "img", axis=0, tiled=True)
    slices = gathered[target].reshape(R, KB, 2, BW)
    accumulated, evidence = score_images(images, groups, slices, shifts, ctf)
    acc_rows = accumulated.reshape(block_count, 2 * BW)
    outbound = jnp.zeros((devices * capacity, 2 * BW), jnp.float32).at[target].set(acc_rows)
    received = lax.psum_scatter(outbound, "img", scatter_dimension=0, tiled=True)
    contrib = pick_table(received.reshape(capacity, 2, BW), slot_table, interp, True).reshape(
        capacity, 2 * BW
    )
    new_map = volume.astype(jnp.float32).at[slot_local].add(contrib)
    return (new_map, evidence)


def solution(mesh):
    return jax.shard_map(
        per_device,
        mesh=mesh,
        in_specs=(
            P(("parts", "img"), None),
            P(("parts", "img")),
            P("parts", None),
            P(("parts", "img"), None),
            P("parts", None),
            P("parts"),
            P("parts"),
            P(),
            P("parts", None),
        ),
        out_specs=(P(("parts", "img"), None), P(("parts", "img"))),
        check_vma=False,
    )
```

profile of v0, /device:TPU:0, one launch (start us, length us, event | category | flops | bytes accessed | tf_op | source)
XLA Modules:
  0.0 340.5 jit_solution(2389398079491741984)
XLA Ops:
  8.0 4.6 %reduce-window.6 = s32[16,32,128]{2,1,0:T(8,128)S(1)} reduce-window(s32[16,32,128]{2,1,0:T(8,128)S(1)} %fusion.140, s32[]{:T(128)} %constant.18.clone.1), window={size=1x1x128 pad=0_0x0_0x127_0}, to_apply=%region_0.0 | reduce-window | flops 8323072 | bytes 524292 | tf_op jit(solution)/shard_map/reduce-window
  15.2 15.5 %scatter_custom_fusion = s32[384]{0:T(512)S(1)} fusion(s32[4096]{0:T(1024)S(1)} %bitcast.279, s32[4096]{0:T(1024)S(1)} %iota.31, s32[]{:T(128)} %constant.16.clone.1), kind=kCustom, calls=%fused_computation.224 | custom fusion | bytes 1540 | tf_op jit(solution)/shard_map/scatter | solution.py:113
  31.4 2.5 gather_fusion
  36.6 2.5 gather_fusion.2
  40.8 5.2 %reshape.246 = f32[64,64,2,128]{3,2,1,0:T(2,128)} reshape(bf16[64,16384]{1,0:T(8,128)(2,1)S(1)} %copy-done.5) | data formatting | bytes 6291456 | tf_op jit(solution)/shard_map/reshape | solution.py:53
  48.3 3.5 %mul.700.clone = f32[64,64,2,128]{3,2,1,0:T(2,128)} broadcast(f32[64,64,128]{2,1,0:T(8,128)S(1)} %bitcast.267), dimensions={0,1,3} | broadcast | bytes 6291456 | tf_op jit(solution)/shard_map/mul | solution.py:53
  51.7 6.5 %mul.795 = f32[64,16384]{1,0:T(8,128)} reshape(f32[64,64,2,128]{3,2,1,0:T(2,128)} %mul.700.clone) | data formatting | bytes 8388608 | tf_op jit(solution)/shard_map/mul | solution.py:53
  58.2 3.9 %fusion.12 = bf16[16384,64]{0,1:T(8,128)(2,1)} fusion(f32[64,16384]{1,0:T(8,128)} %mul.795, bf16[64,16384]{1,0:T(8,128)(2,1)S(1)} %copy-done.5), kind=kLoop, calls=%fused_computation.24 | loop fusion | flops 3145728 | bytes 8388608 | tf_op jit(solution)/shard_map/dot_general | solution.py:84
  62.1 3.3 dot_general.87
  71.2 3.8 %fusion.10 = bf16[64,64,2,128]{3,0,2,1:T(8,128)(2,1)} fusion(f32[64,64,2,128]{3,2,1,0:T(2,128)S(1)} %copy-done.3, f32[64,64,128]{2,0,1:T(8,128)S(1)} %copy_bitcast_fusion), kind=kLoop, calls=%fused_computation.19 | loop fusion | flops 2097152 | bytes 8388608 | tf_op jit(solution)/shard_map/convert_element_type | solution.py:54
  75.0 13.6 %all-gather.2.cloned.1.call-done = bf16[6144,256]{1,0:T(8,128)(2,1)} async-done(((bf16[384,256]{1,0:T(8,128)(2,1)}), bf16[6144,256]{1,0:T(8,128)(2,1)}) %all-gather.2.cloned.1.call-update) | async-done | bytes 3145744 | tf_op jit(solution)/shard_map/all_gather | solution.py:125
  88.6 19.5 %gather_fusion.3 = bf16[4096,256]{1,0:T(8,128)(2,1)} fusion(bf16[6144,256]{1,0:T(8,128)(2,1)} %all-gather.2.cloned.1.call-done, s32[4096]{0:T(1024)} %broadcast_clamp_fusion), kind=kCustom, calls=%fused_computation.3 | custom fusion | bytes 4210688 | tf_op jit(solution)/shard_map/gather | solution.py:126
  108.1 5.3 %reshape.250 = f32[64,64,2,128]{3,2,1,0:T(2,128)} reshape(bf16[4096,256]{1,0:T(8,128)(2,1)} %gather_fusion.3) | data formatting | bytes 6291456 | tf_op jit(solution)/shard_map/convert_element_type | solution.py:47
  113.4 7.9 %fusion.177 = (f32[64,64,1,128]{3,2,1,0:T(1,128)S(1)}, f32[64,64,1,128]{3,2,1,0:T(1,128)S(1)}) fusion(f32[64,64,2,128]{3,2,1,0:T(2,128)} %reshape.250), kind=kLoop, calls=%fused_computation.241 | loop fusion | bytes 8388608 | tf_op jit(solution)/shard_map/slice | solution.py:62
  121.4 8.2 %subtract_convert_fusion = (bf16[64,64,1,128]{3,0,2,1:T(8,128)(2,1)S(1)}, bf16[64,64,1,128]{3,0,2,1:T(8,128)(2,1)S(1)}, f32[64,64,1,128]{3,0,2,1:T(8,128)S(1)}, ...) fusion(f32[64,128]{1,0:T(8,128)S(1)} %copy-done.11, ...), kind=kLoop, calls=%fused_computation.84 | loop fusion | flops 35127296 | bytes 23592960 | tf_op jit(solution)/shard_map/convert.1
  130.8 2.5 fusion.13
  133.6 2.7 subtract_convert_fusion.8
  160.8 3.8 %fusion.151 = f32[64,64,2,128]{3,0,2,1:T(8,128)} fusion(bf16[64,2,128,64]{2,1,0,3:T(2,128)(2,1)S(1)} %dot_general.87, bf16[64,9,64]{0,2,1:T(8,128)(2,1)S(1)} %divide_convert_fusion), kind=kOutput, calls=%fused_computation.158 | convolution fusion | flops 134217728 | bytes 6307840 | tf_op jit(solution)/shard_map/dot_general | solution.py:84
  178.3 3.1 multiply_add_fusion.4
  181.5 2.6 multiply_add_fusion.5
  184.0 2.6 multiply_add_fusion
  186.7 2.6 multiply_add_fusion.1
  189.2 2.6 multiply_add_fusion.2
  191.8 2.6 multiply_add_fusion.3
  194.4 2.6 multiply_add_fusion.6
  197.0 2.6 multiply_add_fusion.7
  199.6 2.6 multiply_add_fusion.8
  202.2 12.3 %fusion.9 = f32[64,64,2,128]{3,0,2,1:T(8,128)S(1)} fusion(f32[64,64,1,128]{3,0,2,1:T(8,128)} %get-tuple-element.19, f32[64,64,1,128]{3,0,2,1:T(8,128)} %get-tuple-element.18, f32[64,64,1,128]{3,0,2,1:T(8,128)} %get-tuple-element.17, f32[64,64,1,128]{3,0,2,1:T(8,128)} %get-tuple-element.16, f32[64,64,1,128]{3,0,2,1:T(8,128)} %get-tuple-element.15, ...), kind=kLoop, calls=%fused_computation.17 | loop fusion | flops 17825792 | bytes 41943040 | tf_op jit(solution)/shard_map/add | solution.py:96
  214.5 5.3 %copy.98 = f32[64,64,2,128]{3,2,1,0:T(2,128)} copy(f32[64,64,2,128]{3,0,2,1:T(8,128)S(1)} %fusion.9) | data formatting | bytes 8388608 | tf_op jit(solution)/shard_map/add | solution.py:96
  219.8 22.2 %scatter_custom_fusion.1 = f32[6144,256]{1,0:T(8,128)} fusion(s32[4096]{0:T(1024)S(1)} %bitcast.276, f32[512,8,2,128]{3,2,1,0:T(2,128)} %bitcast.266, f32[]{:T(128)} %constant.8.clone.1), kind=kCustom, calls=%fused_computation.7 | custom fusion | bytes 10485764 | tf_op jit(solution)/shard_map/scatter | solution.py:129
  243.2 83.0 %reduce-scatter.2.cloned.1.call-done = f32[384,256]{1,0:T(8,128)} async-done(((f32[6144,256]{1,0:T(8,128)}), f32[384,256]{1,0:T(8,128)}) %reduce-scatter.2.cloned.1.call-update) | async-done | bytes 393232 | tf_op jit(solution)/shard_map/reduce_scatter | solution.py:130
  329.3 3.1 scatter_fusion
  (138 shorter events, 61.2 us)
Async XLA Ops:
  7.2 32.1 %copy-start = (bf16[8,128,128]{2,1,0:T(8,128)(2,1)S(1)}, bf16[8,128,128]{2,1,0:T(8,128)(2,1)}, u32[]{:S(2)}) copy-start(bf16[8,128,128]{2,1,0:T(8,128)(2,1)} %param.16) | copy-start | bytes 786436
  7.2 81.4 %all-gather.2.cloned.1.call-start = ((), (), s32[]{:S(2)}) async-start(), calls=%async_computation.1 | async-start | bytes 3342336 | tf_op jit(solution)/shard_map/all_gather | solution.py:125
  7.2 27.3 %copy-start.4 = (bf16[1024,256]{1,0:T(8,128)(2,1)S(1)}, bf16[1024,256]{1,0:T(8,128)(2,1)}, u32[]{:S(2)}) copy-start(bf16[1024,256]{1,0:T(8,128)(2,1)} %param.12) | copy-start | bytes 1572868
  39.2 1.6 copy-start.5
  39.2 1.3 copy-start.25
  40.6 5.4 %copy-start.8 = (f32[8,8192]{1,0:T(8,128)S(1)}, f32[8,8192]{1,0:T(8,128)}, u32[]{:S(2)}) copy-start(f32[8,8192]{1,0:T(8,128)} %param.17) | copy-start | bytes 786436
  40.6 5.4 %copy-start.32 = (s32[64]{0:T(128)S(1)}, s32[64]{0:T(128)}, u32[]{:S(2)}) copy-start(s32[64]{0:T(128)} %param.10) | copy-start | bytes 772
  40.6 285.6 %reduce-scatter.2.cloned.1.call-start = ((), (), s32[]{:S(2)}) async-start(), calls=%async_computation.2 | async-start | bytes 6684672 | tf_op jit(solution)/shard_map/reduce_scatter | solution.py:130
  47.0 1.3 copy-start.1
  62.1 3.3 copy-start.31
  68.0 53.3 %copy-start.9 = (f32[64,128]{1,0:T(8,128)}, f32[64,128]{1,0:T(8,128)S(1)}, u32[]{:S(2)}) copy-start(f32[64,128]{1,0:T(8,128)S(1)} %get-tuple-element.106) | copy-start | bytes 98308
  68.0 3.2 copy-start.3
  113.3 8.0 %copy-start.11 = (f32[64,128]{1,0:T(8,128)S(1)}, f32[64,128]{1,0:T(8,128)}, u32[]{:S(2)}) copy-start(f32[64,128]{1,0:T(8,128)} %get-tuple-element.64) | copy-start | bytes 98308
  113.4 8.0 %copy-start.13 = (f32[64,128]{1,0:T(8,128)S(1)}, f32[64,128]{1,0:T(8,128)}, u32[]{:S(2)}) copy-start(f32[64,128]{1,0:T(8,128)} %get-tuple-element.107) | copy-start | bytes 98308
  113.4 8.0 %copy-start.15 = (f32[64,128]{1,0:T(8,128)S(1)}, f32[64,128]{1,0:T(8,128)}, u32[]{:S(2)}) copy-start(f32[64,128]{1,0:T(8,128)} %get-tuple-element.69) | copy-start | bytes 98308
  113.4 8.0 %copy-start.17 = (f32[64,128]{1,0:T(8,128)S(1)}, f32[64,128]{1,0:T(8,128)}, u32[]{:S(2)}) copy-start(f32[64,128]{1,0:T(8,128)} %get-tuple-element.102) | copy-start | bytes 98308
  113.4 8.0 %copy-start.19 = (f32[64,128]{1,0:T(8,128)S(1)}, f32[64,128]{1,0:T(8,128)}, u32[]{:S(2)}) copy-start(f32[64,128]{1,0:T(8,128)} %get-tuple-element.68) | copy-start | bytes 98308
  113.4 8.0 %copy-start.21 = (f32[64,128]{1,0:T(8,128)S(1)}, f32[64,128]{1,0:T(8,128)}, u32[]{:S(2)}) copy-start(f32[64,128]{1,0:T(8,128)} %get-tuple-element.103) | copy-start | bytes 98308
  130.8 2.6 copy-start.33
  133.6 2.7 copy-start.7
  160.6 4.0 %copy-start.27 = (f32[64]{0:T(128)}, f32[64]{0:T(128)S(1)}, u32[]{:S(2)}) copy-start(f32[64]{0:T(128)S(1)} %maximum_maximum_fusion) | copy-start | bytes 772
  160.7 3.9 %copy-start.29 = (f32[64]{0:T(128)}, f32[64]{0:T(128)S(1)}, u32[]{:S(2)}) copy-start(f32[64]{0:T(128)S(1)} %fusion.141) | copy-start | bytes 772
  176.6 1.7 copy-start.20
  176.6 1.7 copy-start.22
  178.3 3.1 copy-start.16
  178.3 3.1 copy-start.18
  181.4 2.6 copy-start.12
  181.4 2.6 copy-start.14
  184.0 2.6 copy-start.10
  199.6 2.6 copy-start.6
  242.0 85.4 %copy-start.26 = (f32[384,8]{0,1:T(8,128)S(1)}, f32[384,8]{0,1:T(8,128)}, u32[]{:S(2)}) copy-start(f32[384,8]{0,1:T(8,128)} %copy-done.25) | copy-start | bytes 36868
  242.6 86.6 %copy-start.24 = (s32[384]{0:T(512)S(1)}, s32[384]{0:T(512)}, u32[]{:S(2)}) copy-start(s32[384]{0:T(512)} %copy-done.23) | copy-start | bytes 4612
  (4 other events, 2.8 us)
Sparse Core Ops, SparseCore 0:
  40.7 47.8 all-gather.1
  242.1 84.0 reduce-scatter.1
where the time goes:
time: 346 us; the launch traced here: 340 us
  local copies, waits for them, and re-layouts  112 us (32%)
  waiting for transfers between devices  96.7 us (28%)
  other arithmetic  81.3 us (23%)
  matrix products  35.1 us (10%)
  between operations  14.9 us (4%)
    reduce_scatter x1, waiting for transfers between devices, per_device(): lax.psum_scatter(outbound, 'img', scatter_dimension=0, tiled=True)  83 us
    add x9, other arithmetic, score_images(): partial_sum[:, :, 0] * cosine[number]  23.8 us
    scatter x1, local copies, waits for them, and re-layouts, per_device(): jnp.zeros((devices * capacity, 2 * BW), jnp.float32).at[target]  22.2 us
    gather x1, local copies, waits for them, and re-layouts, per_device(): slices = gathered[target].reshape(R, KB, 2, BW)  19.5 us
    dot_general x9, matrix products, score_images(): lax.dot_general(weights[:, number, :], weighted, (((0,), (0,)), ((), ()))...  17.4 us
    another operation x5, other arithmetic  15.8 us
    scatter x1, local copies, waits for them, and re-layouts, per_device(): slot_source = jnp.full((capacity,), block_count, jnp.int32).at[jnp.where(...  15.5 us
    all_gather x1, waiting for transfers between devices, per_device(): gathered = lax.all_gather(own_slices, 'img', axis=0, tiled=True)  13.6 us
  transfers between devices with their start and end apart: 2, of which 2 were waited for; matrix products, arithmetic and copies ran while one was open for 10% of the time, Pallas kernels for 0%

commit v1 on v0

v1 whole, which is shorter than its diff:
```python
import functools
import math

import jax
import jax.numpy as jnp
from jax import lax
from jax.experimental import pallas as pl
from jax.experimental.pallas import tpu as pltpu
from jax.sharding import PartitionSpec as P

BW = 128
KB = 64
R = 64
GROUP = 4

exact_mode = lax.Precision.HIGHEST
VMEM = pltpu.VMEM


def phases(shifts):
    freq_x = (jnp.arange(BW) - BW // 2).astype(jnp.float32)
    freq_y = jnp.arange(KB).astype(jnp.float32)
    shift_x = shifts[:, 0].astype(jnp.float32)
    shift_y = shifts[:, 1].astype(jnp.float32)
    angles = (
        2.0
        * math.pi
        / BW
        * (
            shift_x[None, :, None] * freq_x[None, None, :]
            + shift_y[None, :, None] * freq_y[:, None, None]
        )
    )
    return (jnp.cos(angles), jnp.sin(angles))


def thirds(x):
    high = x.astype(jnp.bfloat16)
    rest = x - high.astype(jnp.float32)
    mid = rest.astype(jnp.bfloat16)
    low = (rest - mid.astype(jnp.float32)).astype(jnp.bfloat16)
    return (high, mid, low)


def prep_kernel(local_ref, table_ref, volume_ref, interp_ref, out_ref):
    count = local_ref.shape[0]
    blocks = volume_ref.shape[0]
    hot = (
        (local_ref[...] == lax.broadcasted_iota(jnp.int32, (count, blocks), 1))
        .astype(jnp.float32)
        .astype(jnp.bfloat16)
    )
    rows = jnp.dot(hot, volume_ref[...], preferred_element_type=jnp.float32).astype(jnp.bfloat16)
    table = table_ref[...]
    for part in range(2):
        piece = rows[:, part * BW : (part + 1) * BW]
        total = jnp.zeros((count, BW), jnp.float32)
        for t in range(interp_ref.shape[0]):
            value = lax.dot_general(
                piece, interp_ref[t], (((1,), (1,)), ((), ())), preferred_element_type=jnp.float32
            )
            total = jnp.where(table == t, value, total)
        out_ref[:, part * BW : (part + 1) * BW] = total.astype(jnp.bfloat16)


def end_kernel(local_ref, table_ref, real_ref, imag_ref, volume_ref, interp_ref, out_ref):
    count = table_ref.shape[0]
    blocks = volume_ref.shape[0]
    hot = (
        (local_ref[...] == lax.broadcasted_iota(jnp.int32, (blocks, count), 0))
        .astype(jnp.float32)
        .astype(jnp.bfloat16)
    )
    table = table_ref[...]
    for part, received_ref in enumerate((real_ref, imag_ref)):
        cols = slice(part * BW, (part + 1) * BW)
        total = jnp.zeros((count, BW), jnp.float32)
        pieces = thirds(received_ref[...])
        for t in range(interp_ref.shape[0]):
            value = jnp.zeros((count, BW), jnp.float32)
            for piece in pieces[::-1]:
                value = value + jnp.dot(
                    piece, interp_ref[t], preferred_element_type=jnp.float32
                )
            total = jnp.where(table == t, value, total)
        added = jnp.zeros((blocks, BW), jnp.float32)
        for piece in thirds(total)[::-1]:
            added = added + jnp.dot(hot, piece, preferred_element_type=jnp.float32)
        out_ref[:, cols] = volume_ref[:, cols].astype(jnp.float32) + added


def weight_kernel(images_ref, hot_ref, ctf_ref, out_ref):
    values = jnp.dot(
        hot_ref[...], ctf_ref[...], precision=exact_mode, preferred_element_type=jnp.float32
    )
    for k in range(ctf_ref.shape[1] // BW):
        factor = values[:, k * BW : (k + 1) * BW]
        for part in range(2):
            cols = slice((2 * k + part) * BW, (2 * k + part + 1) * BW)
            out_ref[:, cols] = (images_ref[:, cols].astype(jnp.float32) * factor).astype(
                jnp.bfloat16
            )


def main_kernel(
    target_ref,
    gathered_ref,
    weighted_ref,
    hot_ref,
    ctf_ref,
    cos_ref,
    sin_ref,
    out_real,
    out_imag,
    evidence_ref,
    wide,
    real_rows,
    imag_rows,
    powers,
    rotated,
    scores,
    weights,
):
    shifts = cos_ref.shape[1]
    count = weighted_ref.shape[0]
    slots = gathered_ref.shape[0]
    step = 256

    @pl.loop(0, slots // step)
    def _(i):
        rows = pl.ds(pl.multiple_of(i * step, step), step)
        wide[rows, :] = gathered_ref[rows, :].astype(jnp.float32)
        out_real[rows, :] = jnp.zeros((step, BW), jnp.float32)
        out_imag[rows, :] = jnp.zeros((step, BW), jnp.float32)

    scores[...] = jnp.zeros_like(scores)

    @pl.loop(0, KB // GROUP)
    def _(i):
        for k in range(GROUP):
            b = i * GROUP + k
            for r in range(R):
                row = wide[pl.ds(target_ref[r * KB + b], 1), :]
                real_rows[k, r : r + 1, :] = row[:, :BW]
                imag_rows[k, r : r + 1, :] = row[:, BW:]
        for k in range(GROUP):
            b = i * GROUP + k
            real = real_rows[k]
            imag = imag_rows[k]
            powers[:, pl.ds(pl.multiple_of(b * BW, BW), BW)] = real * real + imag * imag
            for s in range(shifts):
                c = cos_ref[b, s : s + 1, :]
                n = sin_ref[b, s : s + 1, :]
                rows = slice(s * R, (s + 1) * R)
                rotated[rows, 2 * k * BW : (2 * k + 1) * BW] = (real * c - imag * n).astype(
                    jnp.bfloat16
                )
                rotated[rows, (2 * k + 1) * BW : (2 * k + 2) * BW] = (
                    real * n + imag * c
                ).astype(jnp.bfloat16)
        width = GROUP * 2 * BW
        part = weighted_ref[:, pl.ds(pl.multiple_of(i * width, width), width)]
        scores[...] += lax.dot_general(
            rotated[...], part, (((1,), (1,)), ((), ())), preferred_element_type=jnp.float32
        )

    ctf = ctf_ref[...]
    norms = lax.dot_general(
        powers[...],
        ctf * ctf,
        (((1,), (1,)), ((), ())),
        precision=exact_mode,
        preferred_element_type=jnp.float32,
    )
    image_norms = lax.dot_general(
        norms,
        hot_ref[...],
        (((1,), (1,)), ((), ())),
        precision=exact_mode,
        preferred_element_type=jnp.float32,
    )
    scale = 1.0 / math.sqrt(KB * BW)
    values = (scores[...].reshape(shifts, R, count) - 0.5 * image_norms[None]) * scale
    most = jnp.max(jnp.max(values, axis=0), axis=0, keepdims=True)
    exponent = jnp.exp(values - most[None])
    summed = jnp.sum(jnp.sum(exponent, axis=0), axis=0, keepdims=True)
    evidence_ref[...] = most + jnp.log(summed)
    weights[...] = (exponent / summed[None]).astype(jnp.bfloat16).reshape(shifts * R, count)

    @pl.loop(0, KB)
    def _(b):
        part = weighted_ref[:, pl.ds(pl.multiple_of(b * 2 * BW, 2 * BW), 2 * BW)]
        real = jnp.zeros((R, BW), jnp.float32)
        imag = jnp.zeros((R, BW), jnp.float32)
        for s in range(shifts):
            product = jnp.dot(
                weights[s * R : (s + 1) * R, :], part, preferred_element_type=jnp.float32
            )
            c = cos_ref[b, s : s + 1, :]
            n = sin_ref[b, s : s + 1, :]
            real = real + product[:, :BW] * c + product[:, BW:] * n
            imag = imag + product[:, BW:] * c - product[:, :BW] * n
        k = lax.rem(b, 2)
        real_rows[k] = real
        imag_rows[k] = imag
        for r in range(R):
            row = pl.ds(target_ref[r * KB + b], 1)
            out_real[row, :] = real_rows[k, r : r + 1, :]
            out_imag[row, :] = imag_rows[k, r : r + 1, :]


def per_device(images, groups, shifts, volume, owner, local, table_id, interp, ctf):
    devices = lax.axis_size("img")
    myself = lax.axis_index("img")
    block_count = R * KB
    count = images.shape[0]
    blocks = volume.shape[0]
    tries = shifts.shape[0]
    capacity = max(2, 3 * block_count // (2 * devices))
    slots = devices * capacity
    owners = owner[:, 0]

    lines = block_count // BW
    member = (owners[:, None] == jnp.arange(devices, dtype=jnp.int32)[None, :]).astype(jnp.bfloat16)
    member = member.reshape(lines, BW, devices)
    lower = jnp.tril(jnp.ones((BW, BW), jnp.bfloat16))
    within = jnp.einsum("ab,kbn->kan", lower, member, preferred_element_type=jnp.float32)
    before = jnp.dot(
        jnp.tril(jnp.ones((lines, lines), jnp.bfloat16), -1),
        within[:, -1, :].astype(jnp.bfloat16),
        preferred_element_type=jnp.float32,
    )
    rank = jnp.sum((within + before[:, None, :]) * member.astype(jnp.float32), axis=2) - 1.0
    position = rank.reshape(block_count).astype(jnp.int32)
    target = owners * capacity + position

    place = jnp.where(owners == myself, position, capacity)
    chosen = (place[None, :] == jnp.arange(capacity, dtype=jnp.int32)[:, None]).astype(jnp.bfloat16)
    columns = jnp.stack([local // 256, local % 256, table_id], axis=1).astype(jnp.bfloat16)
    slot_info = jnp.dot(chosen, columns, preferred_element_type=jnp.float32).astype(jnp.int32)
    slot_local = slot_info[:, 0] * 256 + slot_info[:, 1]
    slot_table = slot_info[:, 2:3]

    own_slices = pl.pallas_call(
        prep_kernel,
        out_shape=jax.ShapeDtypeStruct((capacity, 2 * BW), jnp.bfloat16),
        name="prep",
    )(slot_local[:, None], slot_table, volume, interp)
    gathered = lax.all_gather(own_slices, "img", axis=0, tiled=True)

    hot = (groups[:, None] == jnp.arange(ctf.shape[0])[None, :]).astype(jnp.float32)
    width = 2048
    weighted = pl.pallas_call(
        weight_kernel,
        out_shape=jax.ShapeDtypeStruct(images.shape, jnp.bfloat16),
        grid=(images.shape[1] // width,),
        in_specs=[
            pl.BlockSpec((count, width), lambda i: (0, i)),
            pl.BlockSpec((count, ctf.shape[0]), lambda i: (0, 0)),
            pl.BlockSpec((ctf.shape[0], width // 2), lambda i: (0, i)),
        ],
        out_specs=pl.BlockSpec((count, width), lambda i: (0, i)),
        cost_estimate=pl.CostEstimate(
            flops=20 * images.size, bytes_accessed=12 * images.size, transcendentals=0
        ),
        name="weight",
    )(images, hot, ctf)
    cosine, sine = phases(shifts)

    out_real, out_imag, evidence = pl.pallas_call(
        main_kernel,
        out_shape=(
            jax.ShapeDtypeStruct((slots, BW), jnp.float32),
            jax.ShapeDtypeStruct((slots, BW), jnp.float32),
            jax.ShapeDtypeStruct((1, count), jnp.float32),
        ),
        in_specs=[pl.BlockSpec(memory_space=pltpu.SMEM)]
        + [pl.BlockSpec(memory_space=VMEM)] * 6,
        out_specs=(pl.BlockSpec(memory_space=VMEM),) * 3,
        scratch_shapes=[
            VMEM((slots, 2 * BW), jnp.float32),
            VMEM((GROUP, R, BW), jnp.float32),
            VMEM((GROUP, R, BW), jnp.float32),
            VMEM((R, KB * BW), jnp.float32),
            VMEM((tries * R, GROUP * 2 * BW), jnp.bfloat16),
            VMEM((tries * R, count), jnp.float32),
            VMEM((tries * R, count), jnp.bfloat16),
        ],
        compiler_params=pltpu.CompilerParams(vmem_limit_bytes=48 << 20),
        name="score",
    )(target, gathered, weighted, hot, ctf, cosine, sine)

    received_real = lax.psum_scatter(out_real, "img", scatter_dimension=0, tiled=True)
    received_imag = lax.psum_scatter(out_imag, "img", scatter_dimension=0, tiled=True)
    new_map = pl.pallas_call(
        end_kernel,
        out_shape=jax.ShapeDtypeStruct((blocks, 2 * BW), jnp.float32),
        name="finish",
    )(slot_local[None, :], slot_table, received_real, received_imag, volume, interp)
    return (new_map, evidence.reshape(count))


def solution(mesh):
    return jax.shard_map(
        per_device,
        mesh=mesh,
        in_specs=(
            P(("parts", "img"), None),
            P(("parts", "img")),
            P("parts", None),
            P(("parts", "img"), None),
            P("parts", None),
            P("parts"),
            P("parts"),
            P(),
            P("parts", None),
        ),
        out_specs=(P(("parts", "img"), None), P(("parts", "img"))),
        check_vma=False,
    )
```

time: 346 us -> 256 us (0.74); the launches traced: 340 us -> 255 us
  local copies, waits for them, and re-layouts: 112 us -> 2.53 us
  waiting for transfers between devices: 96.7 us -> 172 us
  other arithmetic: 81.3 us -> 7.53 us
  Pallas kernels: 0 us -> 56.7 us
  matrix products: 35.1 us -> 2.14 us
    pallas_call x0 -> x4, Pallas kernels: none -> 56.7 us  [the longest x1 41.1 us: per_device(): pl.pallas_call(main_kernel, out_shape=(jax.ShapeDtypeStruct((slots, BW),...]
    reduce_scatter x1 -> x2, waiting for transfers between devices: 83 us -> 133 us  [the longest x1 69 us: per_device(): lax.psum_scatter(out_imag, 'img', scatter_dimension=0, tiled=True)]
    scatter x2 -> x0, local copies, waits for them, and re-layouts: 37.7 us -> none  [the longest x1 22.2 us: per_device(): jnp.zeros((devices * capacity, 2 * BW), jnp.float32).at[target]]
    add x11 -> x3, other arithmetic: 36.6 us -> 0.91 us  [the longest x1 0.89 us: per_device(): slot_local = slot_info[:, 0] * 256 + slot_info[:, 1]]
    dot_general x23 -> x3, matrix products: 35.1 us -> 2.14 us  [the longest x1 1.05 us: per_device(): jnp.dot(chosen, columns, preferred_element_type=jnp.float32)]
    gather x4 -> x0, local copies, waits for them, and re-layouts: 26.6 us -> none  [the longest x1 19.5 us: per_device(): slices = gathered[target].reshape(R, KB, 2, BW)]
    all_gather x1, waiting for transfers between devices: 13.6 us -> 38.6 us  [per_device(): gathered = lax.all_gather(own_slices, 'img', axis=0, tiled=True)]
    another operation x5 -> x3, other arithmetic: 15.8 us -> 1.49 us
  transfers between devices with their start and end apart: 2 -> 3, of which waited for: 2 -> 3; matrix products, arithmetic and copies ran while one was open for 10% -> 1% of each run, Pallas kernels for 0% -> 3%
where the time goes in v1:
time: 256 us; the launch traced here: 255 us
  waiting for transfers between devices  172 us (67%)
  Pallas kernels  56.7 us (22%)
  between operations  13.9 us (5%)
  other arithmetic  7.53 us (3%)
    reduce_scatter x1, waiting for transfers between devices, per_device(): lax.psum_scatter(out_imag, 'img', scatter_dimension=0, tiled=True)  69 us
    reduce_scatter x1, waiting for transfers between devices, per_device(): lax.psum_scatter(out_real, 'img', scatter_dimension=0, tiled=True)  63.9 us
    pallas_call x1, Pallas kernels, per_device(): pl.pallas_call(main_kernel, out_shape=(jax.ShapeDtypeStruct((slots, BW),...  41.1 us
    all_gather x1, waiting for transfers between devices, per_device(): gathered = lax.all_gather(own_slices, 'img', axis=0, tiled=True)  38.6 us
    pallas_call x1, Pallas kernels, per_device(): pl.pallas_call(weight_kernel, out_shape=jax.ShapeDtypeStruct(images.shape...  6.91 us
    pallas_call x1, Pallas kernels, per_device(): pl.pallas_call(end_kernel, out_shape=jax.ShapeDtypeStruct((blocks, 2 * BW...  5.37 us
  transfers between devices with their start and end apart: 3, of which 3 were waited for; matrix products, arithmetic and copies ran while one was open for 1% of the time, Pallas kernels for 3%

profile of v1, /device:TPU:0, one launch (start us, length us, event | category | flops | bytes accessed | tf_op | source)
XLA Modules:
  0.0 255.1 jit_solution(10614274297282368142)
XLA Ops:
  7.2 0.0 all-gather.2.cloned.1.call-start
  7.2 0.7 broadcast_multiply_fusion.1
  8.0 0.8 compare_reduce_fusion
  8.7 0.7 convert.18
  9.5 0.7 fusion.18
  10.3 0.9 fusion.7
  11.2 0.1 slice.25
  11.3 0.0 copy-start.4
  11.3 0.2 copy.13
  11.5 0.2 fusion.25
  11.7 0.9 fusion.5
  12.6 1.0 fusion.2
  13.7 0.9 fusion.36
  14.6 3.3 %prep.1 = bf16[384,256]{1,0:T(8,128)(2,1)} custom-call(s32[384,1]{1,0:T(8,128)} %get-tuple-element.9.local_ref, s32[384,1]{1,0:T(8,128)} %get-tuple-element.10.table_ref, bf16[1024,256]{1,0:T(8,128)(2,1)} %volume_ref.3, bf16[8,128,128]{2,1,0:T(8,128)(2,1)} %interp_ref.3), custom_call_target="tpu_custom_call" | custom-call | tf_op jit(solution)/shard_map/prep/pallas_call | solution.py:244
  17.8 0.0 all-gather.2.cloned.1.call-update
  17.9 0.0 reduce-scatter.3.cloned.1.call-start
  17.9 0.0 copy-done.4
  17.9 0.7 fusion.17.hot_ref
  18.6 6.9 %weight.1.weighted_ref = bf16[64,16384]{1,0:T(8,128)(2,1)} custom-call(bf16[64,16384]{1,0:T(8,128)(2,1)} %images_ref.1, f32[64,8]{1,0:T(8,128)} %fusion.17.hot_ref, f32[8,8192]{1,0:T(8,128)} %ctf_ref.3), custom_call_target="tpu_custom_call" | custom-call | flops 20971520 | bytes 12582912 | tf_op jit(solution)/shard_map/weight/pallas_call | solution.py:253
  25.6 0.1 broadcast_multiply_fusion.2
  25.6 0.1 broadcast_multiply_fusion
  25.7 1.9 fusion.3
  27.6 38.6 %all-gather.2.cloned.1.call-done.gathered_ref = bf16[6144,256]{1,0:T(8,128)(2,1)} async-done(((bf16[384,256]{1,0:T(8,128)(2,1)}), bf16[6144,256]{1,0:T(8,128)(2,1)}) %all-gather.2.cloned.1.call-update) | async-done | bytes 3145744 | tf_op jit(solution)/shard_map/all_gather | solution.py:249
  66.2 1.6 copy-done
  67.8 41.1 %score.1 = (f32[6144,128]{1,0:T(8,128)}, f32[6144,128]{1,0:T(8,128)}, f32[1,64]{1,0:T(1,128)}) custom-call(s32[4096]{0:T(1024)S(1)} %get-tuple-element.13.target_ref, bf16[6144,256]{1,0:T(8,128)(2,1)} %all-gather.2.cloned.1.call-done.gathered_ref, bf16[64,16384]{1,0:T(8,128)(2,1)S(1)} %copy-done, f32[64,8]{1,0:T(8,128)S(1)} %copy-done.2, ...), custom_call_target="tpu_custom_call" | custom-call | tf_op jit(solution)/shard_map/score/pallas_call | solution.py:270
  108.9 0.0 reduce-scatter.3.cloned.1.call-update
  109.0 0.0 reduce-scatter.5.cloned.1.call-start
  109.0 0.7 reduce-scatter.5.cloned.1.call-update
  109.7 0.6 add.76.local_ref
  110.3 63.9 %reduce-scatter.3.cloned.1.call-done.real_ref = f32[384,128]{1,0:T(8,128)} async-done(((f32[6144,128]{1,0:T(8,128)}), f32[384,128]{1,0:T(8,128)}) %reduce-scatter.3.cloned.1.call-update) | async-done | bytes 196624 | tf_op jit(solution)/shard_map/reduce_scatter | solution.py:293
  174.2 69.0 %reduce-scatter.5.cloned.1.call-done.imag_ref = f32[384,128]{1,0:T(8,128)} async-done(((f32[6144,128]{1,0:T(8,128)}), f32[384,128]{1,0:T(8,128)}) %reduce-scatter.5.cloned.1.call-update) | async-done | bytes 196624 | tf_op jit(solution)/shard_map/reduce_scatter | solution.py:294
  243.2 5.4 %finish.1 = f32[1024,256]{1,0:T(8,128)} custom-call(s32[1,384]{1,0:T(1,128)} %add.76.local_ref, s32[384,1]{1,0:T(8,128)} %get-tuple-element.10.table_ref, f32[384,128]{1,0:T(8,128)} %reduce-scatter.3.cloned.1.call-done.real_ref, f32[384,128]{1,0:T(8,128)} %reduce-scatter.5.cloned.1.call-done.imag_ref, bf16[1024,256]{1,0:T(8,128)(2,1)} %volume_ref.3, ...), custom_call_target="tpu_custom_call" | custom-call | tf_op jit(solution)/shard_map/finish/pallas_call | solution.py:295
  (16 shorter events, 0.1 us)
Async XLA Ops:
  7.2 59.1 %all-gather.2.cloned.1.call-start = ((), (), s32[]{:S(2)}) async-start(), calls=%async_computation.2 | async-start | bytes 3342336 | tf_op jit(solution)/shard_map/all_gather | solution.py:249
  11.3 6.6 %copy-start.4 = (s32[64]{0:T(128)S(1)}, s32[64]{0:T(128)}, u32[]{:S(2)}) copy-start(s32[64]{0:T(128)} %param.10) | copy-start | bytes 772
  14.6 11.0 %copy-start.3 = (s32[9,2]{0,1:T(2,128)S(1)}, s32[9,2]{0,1:T(2,128)}, u32[]{:S(2)}) copy-start(s32[9,2]{0,1:T(2,128)} %param.11) | copy-start | bytes 220
  17.8 48.4 %copy-start.1 = (f32[8,8192]{1,0:T(8,128)S(1)}, f32[8,8192]{1,0:T(8,128)}, u32[]{:S(2)}) copy-start(f32[8,8192]{1,0:T(8,128)} %ctf_ref.3) | copy-start | bytes 786436
  17.9 156.3 %reduce-scatter.3.cloned.1.call-start = ((), (), s32[]{:S(2)}) async-start(), calls=%async_computation.3 | async-start | bytes 3342336 | tf_op jit(solution)/shard_map/reduce_scatter | solution.py:293
  18.6 47.6 %copy-start.2 = (f32[64,8]{1,0:T(8,128)S(1)}, f32[64,8]{1,0:T(8,128)}, u32[]{:S(2)}) copy-start(f32[64,8]{1,0:T(8,128)} %fusion.17.hot_ref) | copy-start | bytes 6148
  66.2 1.6 copy-start
  109.0 134.2 %reduce-scatter.5.cloned.1.call-start = ((), (), s32[]{:S(2)}) async-start(), calls=%async_computation.4 | async-start | bytes 3342336 | tf_op jit(solution)/shard_map/reduce_scatter | solution.py:294
Sparse Core Ops, SparseCore 0:
  18.0 48.1 all-gather.1
  109.1 65.0 reduce-scatter.2
  178.0 65.1 reduce-scatter.4

commit v2 on v1

--- a/solution.py
+++ b/solution.py
@@ -209,6 +209,235 @@
             out_imag[row, :] = imag_rows[k, r : r + 1, :]
 
 
+def split_axes(devices):
+    pairs = devices // 2
+    middle = 1
+    while 4 * middle * middle <= pairs:
+        middle *= 2
+    return pairs // middle, middle
+
+
+def place_of(devices):
+    outer, middle = split_axes(devices)
+    me = lax.axis_index("img")
+    return outer, middle, me // (2 * middle), (me // 2) % middle, me % 2
+
+
+def greet(outer, middle, a, b, c, device):
+    barrier = pltpu.get_barrier_semaphore()
+    peers = [device((a + d) % outer, b, c) for d in range(1, outer)]
+    peers += [device(a, (b + d) % middle, c) for d in range(1, middle)]
+    peers += [device(a, b, 1 - c)]
+    for peer in peers:
+        pl.semaphore_signal(
+            barrier, inc=1, device_id={"img": peer}, device_id_type=pl.DeviceIdType.MESH
+        )
+    pl.semaphore_wait(barrier, len(peers))
+
+
+def spread_kernel(devices, own_ref, out_ref, sem_a, sem_b, sem_c, sem_own):
+    outer, middle, a, b, c = place_of(devices)
+
+    def device(a, b, c):
+        return (a * middle + b) * 2 + c
+
+    def slot(a, b, c):
+        return (c * middle + b) * outer + a
+
+    def send(src, where, sems, peer):
+        copy = pltpu.make_async_remote_copy(
+            src_ref=src,
+            dst_ref=out_ref.at[where],
+            send_sem=sems[0],
+            recv_sem=sems[1],
+            device_id={"img": peer},
+            device_id_type=pl.DeviceIdType.MESH,
+        )
+        copy.start()
+        return copy
+
+    greet(outer, middle, a, b, c, device)
+    keep = pltpu.make_async_copy(own_ref, out_ref.at[slot(a, b, c)], sem_own)
+    keep.start()
+    first, second, third = {}, {}, {}
+
+    def to_core(da, db):
+        where = slot((a - da + outer) % outer, (b - db + middle) % middle, c)
+        src = own_ref if da == 0 and db == 0 else out_ref.at[where]
+        sems = (sem_c.at[0, da, db], sem_c.at[1, da, db])
+        third[da, db] = send(src, where, sems, device(a, b, 1 - c))
+
+    def to_middle(da):
+        where = slot((a - da + outer) % outer, b, c)
+        src = own_ref if da == 0 else out_ref.at[where]
+        for db in range(1, middle):
+            sems = (sem_b.at[0, da, db], sem_b.at[1, da, db])
+            second[da, db] = send(src, where, sems, device(a, (b + db) % middle, c))
+
+    here = slot(a, b, c)
+    to_middle(0)
+    for d in range(1, outer):
+        first[d] = send(
+            own_ref, here, (sem_a.at[0, d], sem_a.at[1, d]), device((a + d) % outer, b, c)
+        )
+    to_core(0, 0)
+    for db in range(1, middle):
+        second[0, db].wait_recv()
+        to_core(0, db)
+    for d in sorted(range(1, outer), key=lambda d: min(d, outer - d)):
+        first[d].wait_recv()
+        to_middle(d)
+        to_core(d, 0)
+    for d in range(1, outer):
+        for db in range(1, middle):
+            second[d, db].wait_recv()
+            to_core(d, db)
+    keep.wait()
+    for copy in list(first.values()) + list(second.values()):
+        copy.wait_send()
+    for copy in third.values():
+        copy.wait()
+
+
+def collect_kernel(
+    devices,
+    real_ref,
+    imag_ref,
+    out_real,
+    out_imag,
+    core_box,
+    middle_out,
+    middle_box,
+    outer_out,
+    outer_box,
+    sem_c,
+    sem_b,
+    sem_a,
+):
+    outer, middle, a, b, c = place_of(devices)
+    inputs = (real_ref, imag_ref)
+
+    def device(a, b, c):
+        return (a * middle + b) * 2 + c
+
+    def send(src, dst, sems, peer):
+        copy = pltpu.make_async_remote_copy(
+            src_ref=src,
+            dst_ref=dst,
+            send_sem=sems[0],
+            recv_sem=sems[1],
+            device_id={"img": peer},
+            device_id_type=pl.DeviceIdType.MESH,
+        )
+        copy.start()
+        return copy
+
+    greet(outer, middle, a, b, c, device)
+    order = list(range(1, middle)) + [0]
+    first, second, third = {}, {}, {}
+    for db in order:
+        bq = (b + db) % middle
+        for part in range(2):
+            first[db, part] = send(
+                inputs[part].at[1 - c, bq],
+                core_box.at[db, part],
+                (sem_c.at[0, db, part], sem_c.at[1, db, part]),
+                device(a, b, 1 - c),
+            )
+
+    def pair_sum(db, da, part):
+        bq = (b + db) % middle
+        aq = (a + da) % outer
+        return inputs[part][c, bq, aq] + core_box[db, part, aq]
+
+    steps = list(range(1, outer)) + [0]
+    for db in range(1, middle):
+        first[db, 0].wait_recv()
+        first[db, 1].wait_recv()
+        for da in steps:
+            for part in range(2):
+                middle_out[db - 1, da, part] = pair_sum(db, da, part).astype(jnp.bfloat16)
+            second[db, da] = send(
+                middle_out.at[db - 1, da],
+                middle_box.at[db - 1, da],
+                (sem_b.at[0, db, da], sem_b.at[1, db, da]),
+                device(a, (b + db) % middle, c),
+            )
+    first[0, 0].wait_recv()
+    first[0, 1].wait_recv()
+    outs = (out_real, out_imag)
+    for da in steps:
+        for db in range(1, middle):
+            second[db, da].wait_recv()
+        for part in range(2):
+            total = pair_sum(0, da, part)
+            for db in range(1, middle):
+                total = total + middle_box[db - 1, da, part].astype(jnp.float32)
+            if da:
+                outer_out[da - 1, part] = total.astype(jnp.bfloat16)
+            else:
+                outs[part][...] = total
+        if da:
+            third[da] = send(
+                outer_out.at[da - 1],
+                outer_box.at[da - 1],
+                (sem_a.at[0, da], sem_a.at[1, da]),
+                device((a + da) % outer, b, c),
+            )
+    for da in range(1, outer):
+        third[da].wait_recv()
+        for part in range(2):
+            outs[part][...] += outer_box[da - 1, part].astype(jnp.float32)
+    for copy in list(first.values()) + list(second.values()) + list(third.values()):
+        copy.wait_send()
+
+
+def spread(own, devices):
+    outer, middle = split_axes(devices)
+    return pl.pallas_call(
+        functools.partial(spread_kernel, devices),
+        out_shape=jax.ShapeDtypeStruct((devices,) + own.shape, own.dtype),
+        in_specs=[pl.BlockSpec(memory_space=VMEM)],
+        out_specs=pl.BlockSpec(memory_space=VMEM),
+        scratch_shapes=[
+            pltpu.SemaphoreType.DMA((2, outer)),
+            pltpu.SemaphoreType.DMA((2, outer, middle)),
+            pltpu.SemaphoreType.DMA((2, outer, middle)),
+            pltpu.SemaphoreType.DMA,
+        ],
+        compiler_params=pltpu.CompilerParams(
+            collective_id=0, has_side_effects=True, vmem_limit_bytes=16 << 20
+        ),
+        name="spread",
+    )(own)
+
+
+def collect(real, imag, devices, capacity):
+    outer, middle = split_axes(devices)
+    shape = (2, middle, outer, capacity, BW)
+    most = max(1, middle - 1)
+    return pl.pallas_call(
+        functools.partial(collect_kernel, devices),
+        out_shape=(jax.ShapeDtypeStruct((capacity, BW), jnp.float32),) * 2,
+        in_specs=[pl.BlockSpec(memory_space=VMEM)] * 2,
+        out_specs=(pl.BlockSpec(memory_space=VMEM),) * 2,
+        scratch_shapes=[
+            VMEM((middle, 2, outer, capacity, BW), jnp.float32),
+            VMEM((most, outer, 2, capacity, BW), jnp.bfloat16),
+            VMEM((most, outer, 2, capacity, BW), jnp.bfloat16),
+            VMEM((max(1, outer - 1), 2, capacity, BW), jnp.bfloat16),
+            VMEM((max(1, outer - 1), 2, capacity, BW), jnp.bfloat16),
+            pltpu.SemaphoreType.DMA((2, middle, 2)),
+            pltpu.SemaphoreType.DMA((2, middle, outer)),
+            pltpu.SemaphoreType.DMA((2, outer)),
+        ],
+        compiler_params=pltpu.CompilerParams(
+            collective_id=1, has_side_effects=True, vmem_limit_bytes=40 << 20
+        ),
+        name="collect",
+    )(real.reshape(shape), imag.reshape(shape))
+
+
 def per_device(images, groups, shifts, volume, owner, local, table_id, interp, ctf):
     devices = lax.axis_size("img")
     myself = lax.axis_index("img")
@@ -232,7 +461,9 @@
     )
     rank = jnp.sum((within + before[:, None, :]) * member.astype(jnp.float32), axis=2) - 1.0
     position = rank.reshape(block_count).astype(jnp.int32)
-    target = owners * capacity + position
+    outer, middle = split_axes(devices)
+    ordered = ((owners % 2) * middle + (owners // 2) % middle) * outer + owners // (2 * middle)
+    target = ordered * capacity + position
 
     place = jnp.where(owners == myself, position, capacity)
     chosen = (place[None, :] == jnp.arange(capacity, dtype=jnp.int32)[:, None]).astype(jnp.bfloat16)
@@ -246,7 +477,7 @@
         out_shape=jax.ShapeDtypeStruct((capacity, 2 * BW), jnp.bfloat16),
         name="prep",
     )(slot_local[:, None], slot_table, volume, interp)
-    gathered = lax.all_gather(own_slices, "img", axis=0, tiled=True)
+    gathered = spread(own_slices, devices).reshape(slots, 2 * BW)
 
     hot = (groups[:, None] == jnp.arange(ctf.shape[0])[None, :]).astype(jnp.float32)
     width = 2048
@@ -290,8 +521,7 @@
         name="score",
     )(target, gathered, weighted, hot, ctf, cosine, sine)
 
-    received_real = lax.psum_scatter(out_real, "img", scatter_dimension=0, tiled=True)
-    received_imag = lax.psum_scatter(out_imag, "img", scatter_dimension=0, tiled=True)
+    received_real, received_imag = collect(out_real, out_imag, devices, capacity)
     new_map = pl.pallas_call(
         end_kernel,
         out_shape=jax.ShapeDtypeStruct((blocks, 2 * BW), jnp.float32),

time: 256 us -> 141 us (0.55)
  waiting for transfers between devices: 172 us -> 0 us
  Pallas kernels: 56.7 us -> 121 us
  between operations: 13.9 us -> 0.78 us
  local copies, waits for them, and re-layouts: 2.53 us -> 7.68 us
    reduce_scatter x2 -> x0, waiting for transfers between devices: 133 us -> none  [the longest x1 69 us: per_device(): lax.psum_scatter(out_imag, 'img', scatter_dimension=0, tiled=True)]
    pallas_call x0 -> x2, Pallas kernels: none -> 64.3 us  [the longest x1 36.1 us: collect(): pl.pallas_call(functools.partial(collect_kernel, devices), out_shape=(jax...]
    all_gather x1 -> x0, waiting for transfers between devices: 38.6 us -> none  [per_device(): gathered = lax.all_gather(own_slices, 'img', axis=0, tiled=True)]
    unnamed x10 -> x18, local copies, waits for them, and re-layouts: 1.61 us -> 6.76 us
  transfers between devices with their start and end apart: 3 -> 0, of which waited for: 3 -> 0; matrix products, arithmetic and copies ran while one was open for 1% -> 0% of each run, Pallas kernels for 3% -> 0%
where the time goes in v2:
time: 141 us; the launch traced here: 140 us
  Pallas kernels  121 us (86%)
  other arithmetic  8.17 us (6%)
  local copies, waits for them, and re-layouts  7.68 us (5%)
  matrix products  2.14 us (2%)
    pallas_call x1, Pallas kernels, per_device(): pl.pallas_call(main_kernel, out_shape=(jax.ShapeDtypeStruct((slots, BW),...  41.2 us
    pallas_call x1, Pallas kernels, collect(): pl.pallas_call(functools.partial(collect_kernel, devices), out_shape=(jax...  36.1 us
    pallas_call x1, Pallas kernels, spread(): pl.pallas_call(functools.partial(spread_kernel, devices), out_shape=jax.S...  28.2 us
    pallas_call x1, Pallas kernels, per_device(): pl.pallas_call(weight_kernel, out_shape=jax.ShapeDtypeStruct(images.shape...  7.12 us
    unnamed x18, local copies, waits for them, and re-layouts  6.76 us
    pallas_call x1, Pallas kernels, per_device(): pl.pallas_call(end_kernel, out_shape=jax.ShapeDtypeStruct((blocks, 2 * BW...  5.37 us
    pallas_call x1, Pallas kernels, per_device(): pl.pallas_call(prep_kernel, out_shape=jax.ShapeDtypeStruct((capacity, 2 *...  3.26 us

profile of v2, /device:TPU:0, one launch (start us, length us, event | category | flops | bytes accessed | tf_op | source)
XLA Modules:
  0.0 140.0 jit_solution(7854435795497435238)
XLA Ops:
  0.7 0.8 convert_bitcast_fusion.2
  1.4 0.1 broadcast_multiply_fusion.1
  1.5 0.7 convert.18
  2.2 0.7 fusion.18
  3.0 0.1 broadcast_multiply_fusion
  3.1 1.3 fusion.17.hot_ref
  4.4 0.9 fusion.7
  5.4 0.1 slice.25
  5.5 0.2 copy.13
  5.7 0.2 fusion.37
  5.9 0.9 fusion.5
  6.8 0.8 fusion.25
  7.5 1.0 fusion.2
  8.6 0.9 fusion.48
  9.5 0.6 add.88.local_ref
  10.0 3.3 %prep.1.own_ref = bf16[384,256]{1,0:T(8,128)(2,1)} custom-call(s32[384,1]{1,0:T(8,128)} %get-tuple-element.13.local_ref, s32[384,1]{1,0:T(8,128)} %get-tuple-element.14.table_ref, bf16[1024,256]{1,0:T(8,128)(2,1)} %volume_ref.3, bf16[8,128,128]{2,1,0:T(8,128)(2,1)} %interp_ref.3), custom_call_target="tpu_custom_call" | custom-call | tf_op jit(solution)/shard_map/prep/pallas_call | solution.py:475
  13.3 1.9 %fusion.3 = (f32[64,9,128]{2,1,0:T(8,128)S(1)}, f32[64,9,128]{2,1,0:T(8,128)S(1)}) fusion(f32[64,9]{1,0:T(8,128)S(1)} %broadcast_multiply_fusion, f32[9,128]{1,0:T(8,128)S(1)} %broadcast_multiply_fusion.1), kind=kLoop, calls=%fused_computation.5 | loop fusion | flops 147456 | bytes 596736 | tf_op jit(solution)/shard_map/sin | solution.py:34
  15.2 0.0 copy-start.4
  15.2 0.0 copy-start.6
  15.2 7.1 %weight.1.weighted_ref = bf16[64,16384]{1,0:T(8,128)(2,1)} custom-call(bf16[64,16384]{1,0:T(8,128)(2,1)} %images_ref.1, f32[64,8]{1,0:T(8,128)} %fusion.17.hot_ref, f32[8,8192]{1,0:T(8,128)} %ctf_ref.3), custom_call_target="tpu_custom_call" | custom-call | flops 20971520 | bytes 12582912 | tf_op jit(solution)/shard_map/weight/pallas_call | solution.py:484
  22.4 0.0 copy-done.5
  22.4 28.2 %spread.1 = bf16[16,384,256]{2,1,0:T(8,128)(2,1)S(1)} custom-call(bf16[384,256]{1,0:T(8,128)(2,1)S(1)} %copy-done.5), custom_call_target="tpu_custom_call" | custom-call | tf_op jit(solution)/shard_map/spread/pallas_call | solution.py:397
  50.6 0.0 copy-start
  50.6 1.6 %copy-done = bf16[16,384,256]{2,1,0:T(8,128)(2,1)} copy-done((bf16[16,384,256]{2,1,0:T(8,128)(2,1)}, bf16[16,384,256]{2,1,0:T(8,128)(2,1)S(1)}, u32[]{:S(2)}) %copy-start) | copy-done | bytes 3145752
  52.2 0.0 copy-done.4
  52.2 41.2 %score.1 = (f32[6144,128]{1,0:T(8,128)}, f32[6144,128]{1,0:T(8,128)}, f32[1,64]{1,0:T(1,128)}) custom-call(s32[4096]{0:T(1024)S(1)} %get-tuple-element.17.target_ref, bf16[6144,256]{1,0:T(8,128)(2,1)} %bitcast.25, bf16[64,16384]{1,0:T(8,128)(2,1)S(1)} %copy-done.1, f32[64,8]{1,0:T(8,128)S(1)} %copy-done.6, f32[8,8192]{1,0:T(8,128)S(1)} %copy-done.4, ...), custom_call_target="tpu_custom_call" | custom-call | tf_op jit(solution)/shard_map/score/pallas_call | solution.py:501
  93.4 1.9 %copy-done.2 = f32[6144,128]{1,0:T(8,128)S(1)} copy-done((f32[6144,128]{1,0:T(8,128)S(1)}, f32[6144,128]{1,0:T(8,128)}, u32[]{:S(2)}) %copy-start.2) | copy-done | bytes 3145752
  95.3 1.9 %copy-done.3 = f32[6144,128]{1,0:T(8,128)S(1)} copy-done((f32[6144,128]{1,0:T(8,128)S(1)}, f32[6144,128]{1,0:T(8,128)}, u32[]{:S(2)}) %copy-start.3) | copy-done | bytes 3145752
  97.2 36.1 %collect.1 = (f32[384,128]{1,0:T(8,128)S(1)}, f32[384,128]{1,0:T(8,128)S(1)}) custom-call(f32[2,2,4,384,128]{4,3,2,1,0:T(8,128)S(1)} %bitcast.26, f32[2,2,4,384,128]{4,3,2,1,0:T(8,128)S(1)} %bitcast.27), custom_call_target="tpu_custom_call" | custom-call | tf_op jit(solution)/shard_map/collect/pallas_call | solution.py:419
  133.2 0.7 copy-done.7
  133.9 0.7 copy-done.8
  134.6 5.4 %finish.1 = f32[1024,256]{1,0:T(8,128)} custom-call(s32[1,384]{1,0:T(1,128)} %add.88.local_ref, s32[384,1]{1,0:T(8,128)} %get-tuple-element.14.table_ref, f32[384,128]{1,0:T(8,128)} %copy-done.7, f32[384,128]{1,0:T(8,128)} %copy-done.8, bf16[1024,256]{1,0:T(8,128)(2,1)} %volume_ref.3, bf16[8,128,128]{2,1,0:T(8,128)(2,1)} %interp_ref.3), custom_call_target="tpu_custom_call" | custom-call | tf_op jit(solution)/shard_map/finish/pallas_call | solution.py:525
  (15 shorter events, 0.1 us)
Async XLA Ops:
  13.3 9.1 %copy-start.5 = (bf16[384,256]{1,0:T(8,128)(2,1)S(1)}, bf16[384,256]{1,0:T(8,128)(2,1)}, u32[]{:S(2)}) copy-start(bf16[384,256]{1,0:T(8,128)(2,1)} %prep.1.own_ref) | copy-start | bytes 589828
  15.2 37.0 %copy-start.4 = (f32[8,8192]{1,0:T(8,128)S(1)}, f32[8,8192]{1,0:T(8,128)}, u32[]{:S(2)}) copy-start(f32[8,8192]{1,0:T(8,128)} %ctf_ref.3) | copy-start | bytes 786436
  15.2 37.0 %copy-start.6 = (f32[64,8]{1,0:T(8,128)S(1)}, f32[64,8]{1,0:T(8,128)}, u32[]{:S(2)}) copy-start(f32[64,8]{1,0:T(8,128)} %fusion.17.hot_ref) | copy-start | bytes 6148
  22.4 29.9 %copy-start.1 = (bf16[64,16384]{1,0:T(8,128)(2,1)S(1)}, bf16[64,16384]{1,0:T(8,128)(2,1)}, u32[]{:S(2)}) copy-start(bf16[64,16384]{1,0:T(8,128)(2,1)} %weight.1.weighted_ref) | copy-start | bytes 6291460
  50.6 1.6 %copy-start = (bf16[16,384,256]{2,1,0:T(8,128)(2,1)}, bf16[16,384,256]{2,1,0:T(8,128)(2,1)S(1)}, u32[]{:S(2)}) copy-start(bf16[16,384,256]{2,1,0:T(8,128)(2,1)S(1)} %spread.1) | copy-start | bytes 9437188
  93.4 1.9 %copy-start.2 = (f32[6144,128]{1,0:T(8,128)S(1)}, f32[6144,128]{1,0:T(8,128)}, u32[]{:S(2)}) copy-start(f32[6144,128]{1,0:T(8,128)} %get-tuple-element.7) | copy-start | bytes 9437188
  95.3 1.9 %copy-start.3 = (f32[6144,128]{1,0:T(8,128)S(1)}, f32[6144,128]{1,0:T(8,128)}, u32[]{:S(2)}) copy-start(f32[6144,128]{1,0:T(8,128)} %get-tuple-element.8) | copy-start | bytes 9437188
  133.2 0.7 copy-start.7
  133.9 0.7 copy-start.8

commit v3 on v2

--- a/solution.py
+++ b/solution.py
@@ -42,16 +42,61 @@
     return (high, mid, low)
 
 
-def prep_kernel(local_ref, table_ref, volume_ref, interp_ref, out_ref):
-    count = local_ref.shape[0]
+def prep_kernel(
+    devices, owner_ref, info_ref, volume_ref, interp_ref, out_ref, target_ref, row_ref, table_ref
+):
+    lines = owner_ref.shape[0]
+    count = out_ref.shape[0]
     blocks = volume_ref.shape[0]
-    hot = (
-        (local_ref[...] == lax.broadcasted_iota(jnp.int32, (count, blocks), 1))
-        .astype(jnp.float32)
-        .astype(jnp.bfloat16)
-    )
-    rows = jnp.dot(hot, volume_ref[...], preferred_element_type=jnp.float32).astype(jnp.bfloat16)
-    table = table_ref[...]
+    outer, middle = split_axes(devices)
+    me = lax.axis_index("img")
+    owner = owner_ref[...]
+    bits = jnp.bfloat16
+
+    def one(condition):
+        return jnp.where(condition, 1.0, 0.0).astype(bits)
+
+    def index(shape, axis):
+        return lax.broadcasted_iota(jnp.int32, shape, axis)
+
+    upto = one(index((BW, BW), 0) <= index((BW, BW), 1))
+    earlier = one(index((lines, lines), 1) < index((lines, lines), 0))
+    every = jnp.ones((BW, BW), bits)
+    target = jnp.zeros((lines, BW), jnp.float32)
+    for o in range(devices):
+        mine = one(owner == o)
+        rank = jnp.dot(mine, upto, preferred_element_type=jnp.float32)
+        above = jnp.dot(earlier, mine, preferred_element_type=jnp.float32).astype(bits)
+        rank = rank + jnp.dot(above, every, preferred_element_type=jnp.float32)
+        order = ((o % 2) * middle + (o // 2) % middle) * outer + o // (2 * middle)
+        target = jnp.where(owner == o, rank + (order * count - 1.0), target)
+    target = target.astype(jnp.int32)
+    target_ref[...] = target
+
+    order = ((me % 2) * middle + (me // 2) % middle) * outer + me // (2 * middle)
+    place = target - order * count
+    slot_rows = jnp.zeros((8, count), jnp.float32)
+    slot_columns = jnp.zeros((count, 8), jnp.float32)
+    wanted = index((count, BW), 0)
+    for k in range(lines):
+        chosen = one(place[k : k + 1, :] == wanted)
+        info = info_ref[k].astype(jnp.float32).astype(bits)
+        dims = (((1,), (1,)), ((), ()))
+        slot_rows = slot_rows + lax.dot_general(
+            info, chosen, dims, preferred_element_type=jnp.float32
+        )
+        slot_columns = slot_columns + lax.dot_general(
+            chosen, info, dims, preferred_element_type=jnp.float32
+        )
+    slot_rows = slot_rows.astype(jnp.int32)
+    slot_columns = slot_columns.astype(jnp.int32)
+    row_ref[...] = slot_rows[0:1] * 256 + slot_rows[1:2]
+    local = slot_columns[:, 0:1] * 256 + slot_columns[:, 1:2]
+    table = slot_columns[:, 2:3]
+    table_ref[...] = table
+
+    hot = one(local == index((count, blocks), 1))
+    rows = jnp.dot(hot, volume_ref[...], preferred_element_type=jnp.float32).astype(bits)
     for part in range(2):
         piece = rows[:, part * BW : (part + 1) * BW]
         total = jnp.zeros((count, BW), jnp.float32)
@@ -60,7 +105,7 @@
                 piece, interp_ref[t], (((1,), (1,)), ((), ())), preferred_element_type=jnp.float32
             )
             total = jnp.where(table == t, value, total)
-        out_ref[:, part * BW : (part + 1) * BW] = total.astype(jnp.bfloat16)
+        out_ref[:, part * BW : (part + 1) * BW] = total.astype(bits)
 
 
 def end_kernel(local_ref, table_ref, real_ref, imag_ref, volume_ref, interp_ref, out_ref):
@@ -75,7 +120,7 @@
     for part, received_ref in enumerate((real_ref, imag_ref)):
         cols = slice(part * BW, (part + 1) * BW)
         total = jnp.zeros((count, BW), jnp.float32)
-        pieces = thirds(received_ref[...])
+        pieces = thirds(received_ref[...])[:2]
         for t in range(interp_ref.shape[0]):
             value = jnp.zeros((count, BW), jnp.float32)
             for piece in pieces[::-1]:
@@ -84,19 +129,22 @@
                 )
             total = jnp.where(table == t, value, total)
         added = jnp.zeros((blocks, BW), jnp.float32)
-        for piece in thirds(total)[::-1]:
+        for piece in thirds(total)[1::-1]:
             added = added + jnp.dot(hot, piece, preferred_element_type=jnp.float32)
         out_ref[:, cols] = volume_ref[:, cols].astype(jnp.float32) + added
 
 
-def weight_kernel(images_ref, hot_ref, ctf_ref, out_ref):
-    values = jnp.dot(
-        hot_ref[...], ctf_ref[...], precision=exact_mode, preferred_element_type=jnp.float32
-    )
-    for k in range(ctf_ref.shape[1] // BW):
+def weigh(step, width, images_ref, hot_ref, ctf_ref, out_ref):
+    hot = hot_ref[...].astype(jnp.bfloat16)
+    half = width // 2
+    values = jnp.zeros((images_ref.shape[0], half), jnp.float32)
+    for piece in thirds(ctf_ref[:, pl.ds(pl.multiple_of(step * half, half), half)])[::-1]:
+        values = values + jnp.dot(hot, piece, preferred_element_type=jnp.float32)
+    for k in range(half // BW):
         factor = values[:, k * BW : (k + 1) * BW]
         for part in range(2):
-            cols = slice((2 * k + part) * BW, (2 * k + part + 1) * BW)
+            start = step * width + (2 * k + part) * BW
+            cols = pl.ds(pl.multiple_of(start, BW), BW)
             out_ref[:, cols] = (images_ref[:, cols].astype(jnp.float32) * factor).astype(
                 jnp.bfloat16
             )
@@ -235,7 +283,19 @@
     pl.semaphore_wait(barrier, len(peers))
 
 
-def spread_kernel(devices, own_ref, out_ref, sem_a, sem_b, sem_c, sem_own):
+def spread_kernel(
+    devices,
+    own_ref,
+    images_ref,
+    hot_ref,
+    ctf_ref,
+    out_ref,
+    weighted_ref,
+    sem_a,
+    sem_b,
+    sem_c,
+    sem_own,
+):
     outer, middle, a, b, c = place_of(devices)
 
     def device(a, b, c):
@@ -281,6 +341,13 @@
             own_ref, here, (sem_a.at[0, d], sem_a.at[1, d]), device((a + d) % outer, b, c)
         )
     to_core(0, 0)
+    width = 1024
+    steps = images_ref.shape[1] // width
+
+    @pl.loop(0, steps // 2)
+    def _(i):
+        weigh(i, width, images_ref, hot_ref, ctf_ref, weighted_ref)
+
     for db in range(1, middle):
         second[0, db].wait_recv()
         to_core(0, db)
@@ -288,6 +355,12 @@
         first[d].wait_recv()
         to_middle(d)
         to_core(d, 0)
+        if min(d, outer - d) == 1 and d != 1:
+
+            @pl.loop(steps // 2, steps)
+            def _(i):
+                weigh(i, width, images_ref, hot_ref, ctf_ref, weighted_ref)
+
     for d in range(1, outer):
         for db in range(1, middle):
             second[d, db].wait_recv()
@@ -392,13 +465,16 @@
         copy.wait_send()
 
 
-def spread(own, devices):
+def spread(own, images, hot, ctf, devices):
     outer, middle = split_axes(devices)
     return pl.pallas_call(
         functools.partial(spread_kernel, devices),
-        out_shape=jax.ShapeDtypeStruct((devices,) + own.shape, own.dtype),
-        in_specs=[pl.BlockSpec(memory_space=VMEM)],
-        out_specs=pl.BlockSpec(memory_space=VMEM),
+        out_shape=(
+            jax.ShapeDtypeStruct((devices,) + own.shape, own.dtype),
+            jax.ShapeDtypeStruct(images.shape, images.dtype),
+        ),
+        in_specs=[pl.BlockSpec(memory_space=VMEM)] * 4,
+        out_specs=(pl.BlockSpec(memory_space=VMEM),) * 2,
         scratch_shapes=[
             pltpu.SemaphoreType.DMA((2, outer)),
             pltpu.SemaphoreType.DMA((2, outer, middle)),
@@ -406,10 +482,10 @@
             pltpu.SemaphoreType.DMA,
         ],
         compiler_params=pltpu.CompilerParams(
-            collective_id=0, has_side_effects=True, vmem_limit_bytes=16 << 20
+            collective_id=0, has_side_effects=True, vmem_limit_bytes=24 << 20
         ),
         name="spread",
-    )(own)
+    )(own, images, hot, ctf)
 
 
 def collect(real, imag, devices, capacity):
@@ -440,7 +516,6 @@
 
 def per_device(images, groups, shifts, volume, owner, local, table_id, interp, ctf):
     devices = lax.axis_size("img")
-    myself = lax.axis_index("img")
     block_count = R * KB
     count = images.shape[0]
     blocks = volume.shape[0]
@@ -450,52 +525,23 @@
     owners = owner[:, 0]
 
     lines = block_count // BW
-    member = (owners[:, None] == jnp.arange(devices, dtype=jnp.int32)[None, :]).astype(jnp.bfloat16)
-    member = member.reshape(lines, BW, devices)
-    lower = jnp.tril(jnp.ones((BW, BW), jnp.bfloat16))
-    within = jnp.einsum("ab,kbn->kan", lower, member, preferred_element_type=jnp.float32)
-    before = jnp.dot(
-        jnp.tril(jnp.ones((lines, lines), jnp.bfloat16), -1),
-        within[:, -1, :].astype(jnp.bfloat16),
-        preferred_element_type=jnp.float32,
-    )
-    rank = jnp.sum((within + before[:, None, :]) * member.astype(jnp.float32), axis=2) - 1.0
-    position = rank.reshape(block_count).astype(jnp.int32)
-    outer, middle = split_axes(devices)
-    ordered = ((owners % 2) * middle + (owners // 2) % middle) * outer + owners // (2 * middle)
-    target = ordered * capacity + position
-
-    place = jnp.where(owners == myself, position, capacity)
-    chosen = (place[None, :] == jnp.arange(capacity, dtype=jnp.int32)[:, None]).astype(jnp.bfloat16)
-    columns = jnp.stack([local // 256, local % 256, table_id], axis=1).astype(jnp.bfloat16)
-    slot_info = jnp.dot(chosen, columns, preferred_element_type=jnp.float32).astype(jnp.int32)
-    slot_local = slot_info[:, 0] * 256 + slot_info[:, 1]
-    slot_table = slot_info[:, 2:3]
-
-    own_slices = pl.pallas_call(
-        prep_kernel,
-        out_shape=jax.ShapeDtypeStruct((capacity, 2 * BW), jnp.bfloat16),
+    spare = jnp.zeros((lines, 5, BW), jnp.int32)
+    columns = [x.reshape(lines, 1, BW) for x in (local // 256, local % 256, table_id)]
+    own_slices, target, slot_local, slot_table = pl.pallas_call(
+        functools.partial(prep_kernel, devices),
+        out_shape=(
+            jax.ShapeDtypeStruct((capacity, 2 * BW), jnp.bfloat16),
+            jax.ShapeDtypeStruct((lines, BW), jnp.int32),
+            jax.ShapeDtypeStruct((1, capacity), jnp.int32),
+            jax.ShapeDtypeStruct((capacity, 1), jnp.int32),
+        ),
         name="prep",
-    )(slot_local[:, None], slot_table, volume, interp)
-    gathered = spread(own_slices, devices).reshape(slots, 2 * BW)
+    )(owners.reshape(lines, BW), jnp.concatenate(columns + [spare], axis=1), volume, interp)
+    target = target.reshape(block_count)
 
     hot = (groups[:, None] == jnp.arange(ctf.shape[0])[None, :]).astype(jnp.float32)
-    width = 2048
-    weighted = pl.pallas_call(
-        weight_kernel,
-        out_shape=jax.ShapeDtypeStruct(images.shape, jnp.bfloat16),
-        grid=(images.shape[1] // width,),
-        in_specs=[
-            pl.BlockSpec((count, width), lambda i: (0, i)),
-            pl.BlockSpec((count, ctf.shape[0]), lambda i: (0, 0)),
-            pl.BlockSpec((ctf.shape[0], width // 2), lambda i: (0, i)),
-        ],
-        out_specs=pl.BlockSpec((count, width), lambda i: (0, i)),
-        cost_estimate=pl.CostEstimate(
-            flops=20 * images.size, bytes_accessed=12 * images.size, transcendentals=0
-        ),
-        name="weight",
-    )(images, hot, ctf)
+    gathered, weighted = spread(own_slices, images, hot, ctf, devices)
+    gathered = gathered.reshape(slots, 2 * BW)
     cosine, sine = phases(shifts)
 
     out_real, out_imag, evidence = pl.pallas_call(
@@ -526,7 +572,7 @@
         end_kernel,
         out_shape=jax.ShapeDtypeStruct((blocks, 2 * BW), jnp.float32),
         name="finish",
-    )(slot_local[None, :], slot_table, received_real, received_imag, volume, interp)
+    )(slot_local, slot_table, received_real, received_imag, volume, interp)
     return (new_map, evidence.reshape(count))
 
 

time: 141 us -> 133 us (0.943)
  Pallas kernels: 121 us -> 116 us
  other arithmetic: 8.17 us -> 5.82 us
  matrix products: 2.14 us -> 0 us
  local copies, waits for them, and re-layouts: 7.68 us -> 9.47 us
    pallas_call x3 -> x2, Pallas kernels: 38.6 us -> 34.5 us  [the longest x1 28.1 us: spread(): pl.pallas_call(functools.partial(spread_kernel, devices), out_shape=(jax....]
    unnamed x18 -> x20, local copies, waits for them, and re-layouts: 6.76 us -> 9.39 us
    dot_general x3 -> x0, matrix products: 2.14 us -> none  [the longest x1 1.05 us: per_device(): jnp.dot(chosen, columns, preferred_element_type=jnp.float32)]
    add x3 -> x0, other arithmetic: 1.66 us -> none  [the longest x1 0.89 us: per_device(): slot_local = slot_info[:, 0] * 256 + slot_info[:, 1]]
    another operation x3 -> x0, other arithmetic: 1.48 us -> none
    concatenate x0 -> x1, other arithmetic: none -> 1.45 us  [per_device(): jnp.concatenate(columns + [spare], axis=1)]
where the time goes in v3:
time: 133 us; the launch traced here: 132 us
  Pallas kernels  116 us (87%)
  local copies, waits for them, and re-layouts  9.47 us (7%)
  other arithmetic  5.82 us (4%)
    pallas_call x1, Pallas kernels, per_device(): pl.pallas_call(main_kernel, out_shape=(jax.ShapeDtypeStruct((slots, BW),...  41.2 us
    pallas_call x1, Pallas kernels, collect(): pl.pallas_call(functools.partial(collect_kernel, devices), out_shape=(jax...  36.1 us
    pallas_call x1, Pallas kernels, spread(): pl.pallas_call(functools.partial(spread_kernel, devices), out_shape=(jax....  28.1 us
    unnamed x20, local copies, waits for them, and re-layouts  9.39 us
    pallas_call x1, Pallas kernels, per_device(): pl.pallas_call(functools.partial(prep_kernel, devices), out_shape=(jax.Sh...  6.35 us
    pallas_call x1, Pallas kernels, per_device(): pl.pallas_call(end_kernel, out_shape=jax.ShapeDtypeStruct((blocks, 2 * BW...  4.44 us

profile of v3, /device:TPU:0, one launch (start us, length us, event | category | flops | bytes accessed | tf_op | source)
XLA Modules:
  0.0 132.2 jit_solution(18175441838362949997)
XLA Ops:
  0.6 0.0 copy-start.5
  0.6 0.0 copy-start.3
  0.7 0.1 pad.3.clone
  0.7 0.8 convert_bitcast_fusion.1
  1.6 0.1 broadcast_multiply_fusion.1
  1.7 0.1 broadcast_multiply_fusion
  1.7 0.7 fusion.2.hot_ref
  2.5 0.7 add_select_fusion.1
  3.2 1.5 %add_add_fusion.info_ref = s32[32,8,128]{2,1,0:T(8,128)} fusion(s32[32,1,128]{2,1,0:T(1,128)} %bitcast.20, s32[32,1,128]{2,1,0:T(1,128)S(1)} %bitcast.18, s32[32,1,128]{2,1,0:T(1,128)S(1)} %bitcast.17, s32[8]{0:T(128)S(1)} %pad.3.clone), kind=kLoop, calls=%fused_computation.3 | loop fusion | flops 98304 | bytes 180256 | tf_op jit(solution)/shard_map/concatenate | solution.py:539
  4.7 6.4 %prep.1 = (bf16[384,256]{1,0:T(8,128)(2,1)}, s32[32,128]{1,0:T(8,128)}, s32[1,384]{1,0:T(1,128)}, s32[384,1]{1,0:T(8,128)}) custom-call(s32[32,128]{1,0:T(8,128)} %bitcast.19, s32[32,8,128]{2,1,0:T(8,128)} %add_add_fusion.info_ref, bf16[1024,256]{1,0:T(8,128)(2,1)} %volume_ref.3, bf16[8,128,128]{2,1,0:T(8,128)(2,1)} %interp_ref.3), custom_call_target="tpu_custom_call" | custom-call | tf_op jit(solution)/shard_map/prep/pallas_call | solution.py:530
  11.0 1.9 %fusion = (f32[64,9,128]{2,1,0:T(8,128)S(1)}, f32[64,9,128]{2,1,0:T(8,128)S(1)}) fusion(f32[64,9]{1,0:T(8,128)S(1)} %broadcast_multiply_fusion, f32[9,128]{1,0:T(8,128)S(1)} %broadcast_multiply_fusion.1), kind=kLoop, calls=%fused_computation.1 | loop fusion | flops 147456 | bytes 596736 | tf_op jit(solution)/shard_map/sin | solution.py:34
  12.9 0.0 copy-done.3
  12.9 0.0 copy-start.4
  12.9 0.9 copy-done.4
  13.9 0.0 copy-start.6
  13.9 0.9 copy-done.6
  14.8 28.1 %spread.1 = (bf16[16,384,256]{2,1,0:T(8,128)(2,1)S(1)}, bf16[64,16384]{1,0:T(8,128)(2,1)S(1)}) custom-call(bf16[384,256]{1,0:T(8,128)(2,1)S(1)} %copy-done.6, bf16[64,16384]{1,0:T(8,128)(2,1)S(1)} %copy-done.3, f32[64,8]{1,0:T(8,128)S(1)} %fusion.2.hot_ref, f32[8,8192]{1,0:T(8,128)S(1)} %copy-done.4), custom_call_target="tpu_custom_call" | custom-call | tf_op jit(solution)/shard_map/spread/pallas_call | solution.py:470
  43.0 0.0 copy-start.2
  43.0 1.6 %copy-done.2 = bf16[16,384,256]{2,1,0:T(8,128)(2,1)} copy-done((bf16[16,384,256]{2,1,0:T(8,128)(2,1)}, bf16[16,384,256]{2,1,0:T(8,128)(2,1)S(1)}, u32[]{:S(2)}) %copy-start.2) | copy-done | bytes 3145752
  44.6 0.0 copy-done.5
  44.6 0.0 copy-start.9
  44.6 0.7 copy-done.9
  45.3 41.2 %score.1 = (f32[6144,128]{1,0:T(8,128)}, f32[6144,128]{1,0:T(8,128)}, f32[1,64]{1,0:T(1,128)}) custom-call(s32[4096]{0:T(1024)S(1)} %bitcast.16, bf16[6144,256]{1,0:T(8,128)(2,1)} %bitcast.15, bf16[64,16384]{1,0:T(8,128)(2,1)S(1)} %get-tuple-element.18.weighted_ref, f32[64,8]{1,0:T(8,128)S(1)} %fusion.2.hot_ref, f32[8,8192]{1,0:T(8,128)S(1)} %copy-done.5, ...), custom_call_target="tpu_custom_call" | custom-call | tf_op jit(solution)/shard_map/score/pallas_call | solution.py:547
  86.5 0.0 copy-start
  86.5 1.9 %copy-done = f32[6144,128]{1,0:T(8,128)S(1)} copy-done((f32[6144,128]{1,0:T(8,128)S(1)}, f32[6144,128]{1,0:T(8,128)}, u32[]{:S(2)}) %copy-start) | copy-done | bytes 3145752
  88.4 0.0 copy-start.1
  88.4 1.9 %copy-done.1 = f32[6144,128]{1,0:T(8,128)S(1)} copy-done((f32[6144,128]{1,0:T(8,128)S(1)}, f32[6144,128]{1,0:T(8,128)}, u32[]{:S(2)}) %copy-start.1) | copy-done | bytes 3145752
  90.3 36.1 %collect.1 = (f32[384,128]{1,0:T(8,128)S(1)}, f32[384,128]{1,0:T(8,128)S(1)}) custom-call(f32[2,2,4,384,128]{4,3,2,1,0:T(8,128)S(1)} %bitcast.13, f32[2,2,4,384,128]{4,3,2,1,0:T(8,128)S(1)} %bitcast.14), custom_call_target="tpu_custom_call" | custom-call | tf_op jit(solution)/shard_map/collect/pallas_call | solution.py:495
  126.4 0.0 copy-start.7
  126.4 0.7 copy-done.7
  127.1 0.7 copy-done.8
  127.8 4.4 %finish.1 = f32[1024,256]{1,0:T(8,128)} custom-call(s32[1,384]{1,0:T(1,128)} %get-tuple-element.13.local_ref, s32[384,1]{1,0:T(8,128)} %get-tuple-element.14.table_ref, f32[384,128]{1,0:T(8,128)} %copy-done.7, f32[384,128]{1,0:T(8,128)} %copy-done.8, bf16[1024,256]{1,0:T(8,128)(2,1)} %volume_ref.3, bf16[8,128,128]{2,1,0:T(8,128)(2,1)} %interp_ref.3), custom_call_target="tpu_custom_call" | custom-call | tf_op jit(solution)/shard_map/finish/pallas_call | solution.py:571
  (4 shorter events, 0.0 us)
Async XLA Ops:
  0.6 44.0 %copy-start.5 = (f32[8,8192]{1,0:T(8,128)S(1)}, f32[8,8192]{1,0:T(8,128)}, u32[]{:S(2)}) copy-start(f32[8,8192]{1,0:T(8,128)} %ctf_ref.3) | copy-start | bytes 786436
  0.6 12.3 %copy-start.3 = (bf16[64,16384]{1,0:T(8,128)(2,1)S(1)}, bf16[64,16384]{1,0:T(8,128)(2,1)}, u32[]{:S(2)}) copy-start(bf16[64,16384]{1,0:T(8,128)(2,1)} %images_ref.1) | copy-start | bytes 6291460
  12.9 1.0 copy-start.4
  13.9 0.9 copy-start.6
  43.0 1.7 %copy-start.2 = (bf16[16,384,256]{2,1,0:T(8,128)(2,1)}, bf16[16,384,256]{2,1,0:T(8,128)(2,1)S(1)}, u32[]{:S(2)}) copy-start(bf16[16,384,256]{2,1,0:T(8,128)(2,1)S(1)} %get-tuple-element.17) | copy-start | bytes 9437188
  44.6 0.7 copy-start.9
  86.5 1.9 %copy-start = (f32[6144,128]{1,0:T(8,128)S(1)}, f32[6144,128]{1,0:T(8,128)}, u32[]{:S(2)}) copy-start(f32[6144,128]{1,0:T(8,128)} %get-tuple-element.19) | copy-start | bytes 9437188
  88.4 1.9 %copy-start.1 = (f32[6144,128]{1,0:T(8,128)S(1)}, f32[6144,128]{1,0:T(8,128)}, u32[]{:S(2)}) copy-start(f32[6144,128]{1,0:T(8,128)} %get-tuple-element.20) | copy-start | bytes 9437188
  126.4 0.7 copy-start.7
  127.1 0.7 copy-start.8

commit v4 on v3

--- a/solution.py
+++ b/solution.py
@@ -43,7 +43,7 @@
 
 
 def prep_kernel(
-    devices, owner_ref, info_ref, volume_ref, interp_ref, out_ref, target_ref, row_ref, table_ref
+    devices, owner_ref, local_ref, id_ref, volume_ref, interp_ref, out_ref, target_ref, row_ref, table_ref
 ):
     lines = owner_ref.shape[0]
     count = out_ref.shape[0]
@@ -78,9 +78,16 @@
     slot_rows = jnp.zeros((8, count), jnp.float32)
     slot_columns = jnp.zeros((count, 8), jnp.float32)
     wanted = index((count, BW), 0)
+    locals_ = local_ref[...]
+    high = (locals_ >> 8).astype(jnp.float32)
+    low = (locals_ & 255).astype(jnp.float32)
+    ids = id_ref[...].astype(jnp.float32)
+    blank = jnp.zeros((5, BW), jnp.float32)
     for k in range(lines):
         chosen = one(place[k : k + 1, :] == wanted)
-        info = info_ref[k].astype(jnp.float32).astype(bits)
+        info = jnp.concatenate(
+            [high[k : k + 1], low[k : k + 1], ids[k : k + 1], blank], axis=0
+        ).astype(bits)
         dims = (((1,), (1,)), ((), ()))
         slot_rows = slot_rows + lax.dot_general(
             info, chosen, dims, preferred_element_type=jnp.float32
@@ -158,16 +165,20 @@
     ctf_ref,
     cos_ref,
     sin_ref,
+    keep_ref,
+    send_ref,
+    evidence_ref,
+    wide,
     out_real,
     out_imag,
-    evidence_ref,
-    wide,
     real_rows,
     imag_rows,
     powers,
-    rotated,
+    rotated_even,
+    rotated_odd,
     scores,
     weights,
+    sems,
 ):
     shifts = cos_ref.shape[1]
     count = weighted_ref.shape[0]
@@ -183,18 +194,17 @@
 
     scores[...] = jnp.zeros_like(scores)
 
-    @pl.loop(0, KB // GROUP)
-    def _(i):
+    def turn(i, rotated, first):
         for k in range(GROUP):
             b = i * GROUP + k
             for r in range(R):
                 row = wide[pl.ds(target_ref[r * KB + b], 1), :]
-                real_rows[k, r : r + 1, :] = row[:, :BW]
-                imag_rows[k, r : r + 1, :] = row[:, BW:]
+                real_rows[first + k, r : r + 1, :] = row[:, :BW]
+                imag_rows[first + k, r : r + 1, :] = row[:, BW:]
         for k in range(GROUP):
             b = i * GROUP + k
-            real = real_rows[k]
-            imag = imag_rows[k]
+            real = real_rows[first + k]
+            imag = imag_rows[first + k]
             powers[:, pl.ds(pl.multiple_of(b * BW, BW), BW)] = real * real + imag * imag
             for s in range(shifts):
                 c = cos_ref[b, s : s + 1, :]
@@ -208,9 +218,15 @@
                 ).astype(jnp.bfloat16)
         width = GROUP * 2 * BW
         part = weighted_ref[:, pl.ds(pl.multiple_of(i * width, width), width)]
-        scores[...] += lax.dot_general(
+        return lax.dot_general(
             rotated[...], part, (((1,), (1,)), ((), ())), preferred_element_type=jnp.float32
         )
+
+    @pl.loop(0, KB // GROUP // 2)
+    def _(i):
+        even = turn(2 * i, rotated_even, 0)
+        odd = turn(2 * i + 1, rotated_odd, GROUP)
+        scores[...] += even + odd
 
     ctf = ctf_ref[...]
     norms = lax.dot_general(
@@ -235,8 +251,7 @@
     evidence_ref[...] = most + jnp.log(summed)
     weights[...] = (exponent / summed[None]).astype(jnp.bfloat16).reshape(shifts * R, count)
 
-    @pl.loop(0, KB)
-    def _(b):
+    def back(b, k):
         part = weighted_ref[:, pl.ds(pl.multiple_of(b * 2 * BW, 2 * BW), 2 * BW)]
         real = jnp.zeros((R, BW), jnp.float32)
         imag = jnp.zeros((R, BW), jnp.float32)
@@ -248,13 +263,43 @@
             n = sin_ref[b, s : s + 1, :]
             real = real + product[:, :BW] * c + product[:, BW:] * n
             imag = imag + product[:, BW:] * c - product[:, :BW] * n
-        k = lax.rem(b, 2)
         real_rows[k] = real
         imag_rows[k] = imag
+
+    def place(b, k):
         for r in range(R):
             row = pl.ds(target_ref[r * KB + b], 1)
             out_real[row, :] = real_rows[k, r : r + 1, :]
             out_imag[row, :] = imag_rows[k, r : r + 1, :]
+
+    @pl.loop(0, KB // GROUP)
+    def _(i):
+        for k in range(GROUP):
+            back(i * GROUP + k, k)
+            if k:
+                place(i * GROUP + k - 1, k - 1)
+        place(i * GROUP + GROUP - 1, GROUP - 1)
+
+    half = slots // 2
+    core = lax.axis_index("img") % 2
+    mine = pl.multiple_of(core * half, half)
+    other = pl.multiple_of((1 - core) * half, half)
+    copies = []
+    for part, out in enumerate((out_real, out_imag)):
+        copy = pltpu.make_async_copy(out.at[pl.ds(mine, half)], keep_ref.at[part], sems.at[part])
+        copy.start()
+        copies.append(copy)
+
+    @pl.loop(0, half // step)
+    def _(i):
+        start = pl.multiple_of(i * step, step)
+        for part, out in enumerate((out_real, out_imag)):
+            send_ref[part, pl.ds(start, step), :] = out[
+                pl.ds(pl.multiple_of(other + start, step), step), :
+            ].astype(jnp.bfloat16)
+
+    for copy in copies:
+        copy.wait()
 
 
 def split_axes(devices):
@@ -374,21 +419,22 @@
 
 def collect_kernel(
     devices,
-    real_ref,
-    imag_ref,
+    keep_ref,
+    leave_ref,
     out_real,
     out_imag,
+    own_box,
     core_box,
     middle_out,
     middle_box,
     outer_out,
     outer_box,
+    sem_own,
     sem_c,
     sem_b,
     sem_a,
 ):
     outer, middle, a, b, c = place_of(devices)
-    inputs = (real_ref, imag_ref)
 
     def device(a, b, c):
         return (a * middle + b) * 2 + c
@@ -405,28 +451,35 @@
         copy.start()
         return copy
 
+    order = list(range(1, middle)) + [0]
+    own = {}
+    for db in order:
+        for part in range(2):
+            own[db, part] = pltpu.make_async_copy(
+                keep_ref.at[part, (b + db) % middle], own_box.at[db, part], sem_own.at[db, part]
+            )
+            own[db, part].start()
     greet(outer, middle, a, b, c, device)
-    order = list(range(1, middle)) + [0]
     first, second, third = {}, {}, {}
     for db in order:
         bq = (b + db) % middle
         for part in range(2):
             first[db, part] = send(
-                inputs[part].at[1 - c, bq],
+                leave_ref.at[part, bq],
                 core_box.at[db, part],
                 (sem_c.at[0, db, part], sem_c.at[1, db, part]),
                 device(a, b, 1 - c),
             )
 
     def pair_sum(db, da, part):
-        bq = (b + db) % middle
         aq = (a + da) % outer
-        return inputs[part][c, bq, aq] + core_box[db, part, aq]
+        return own_box[db, part, aq] + core_box[db, part, aq].astype(jnp.float32)
 
     steps = list(range(1, outer)) + [0]
     for db in range(1, middle):
-        first[db, 0].wait_recv()
-        first[db, 1].wait_recv()
+        for part in range(2):
+            own[db, part].wait()
+            first[db, part].wait_recv()
         for da in steps:
             for part in range(2):
                 middle_out[db - 1, da, part] = pair_sum(db, da, part).astype(jnp.bfloat16)
@@ -436,8 +489,9 @@
                 (sem_b.at[0, db, da], sem_b.at[1, db, da]),
                 device(a, (b + db) % middle, c),
             )
-    first[0, 0].wait_recv()
-    first[0, 1].wait_recv()
+    for part in range(2):
+        own[0, part].wait()
+        first[0, part].wait_recv()
     outs = (out_real, out_imag)
     for da in steps:
         for db in range(1, middle):
@@ -488,21 +542,24 @@
     )(own, images, hot, ctf)
 
 
-def collect(real, imag, devices, capacity):
+def collect(keep, leave, devices, capacity):
     outer, middle = split_axes(devices)
     shape = (2, middle, outer, capacity, BW)
+    box = (middle, 2, outer, capacity, BW)
     most = max(1, middle - 1)
     return pl.pallas_call(
         functools.partial(collect_kernel, devices),
         out_shape=(jax.ShapeDtypeStruct((capacity, BW), jnp.float32),) * 2,
-        in_specs=[pl.BlockSpec(memory_space=VMEM)] * 2,
+        in_specs=[pl.BlockSpec(memory_space=pl.ANY)] * 2,
         out_specs=(pl.BlockSpec(memory_space=VMEM),) * 2,
         scratch_shapes=[
-            VMEM((middle, 2, outer, capacity, BW), jnp.float32),
+            VMEM(box, jnp.float32),
+            VMEM(box, jnp.bfloat16),
             VMEM((most, outer, 2, capacity, BW), jnp.bfloat16),
             VMEM((most, outer, 2, capacity, BW), jnp.bfloat16),
             VMEM((max(1, outer - 1), 2, capacity, BW), jnp.bfloat16),
             VMEM((max(1, outer - 1), 2, capacity, BW), jnp.bfloat16),
+            pltpu.SemaphoreType.DMA((middle, 2)),
             pltpu.SemaphoreType.DMA((2, middle, 2)),
             pltpu.SemaphoreType.DMA((2, middle, outer)),
             pltpu.SemaphoreType.DMA((2, outer)),
@@ -511,7 +568,7 @@
             collective_id=1, has_side_effects=True, vmem_limit_bytes=40 << 20
         ),
         name="collect",
-    )(real.reshape(shape), imag.reshape(shape))
+    )(keep.reshape(shape), leave.reshape(shape))
 
 
 def per_device(images, groups, shifts, volume, owner, local, table_id, interp, ctf):
@@ -525,8 +582,6 @@
     owners = owner[:, 0]
 
     lines = block_count // BW
-    spare = jnp.zeros((lines, 5, BW), jnp.int32)
-    columns = [x.reshape(lines, 1, BW) for x in (local // 256, local % 256, table_id)]
     own_slices, target, slot_local, slot_table = pl.pallas_call(
         functools.partial(prep_kernel, devices),
         out_shape=(
@@ -536,7 +591,13 @@
             jax.ShapeDtypeStruct((capacity, 1), jnp.int32),
         ),
         name="prep",
-    )(owners.reshape(lines, BW), jnp.concatenate(columns + [spare], axis=1), volume, interp)
+    )(
+        owners.reshape(lines, BW),
+        local.reshape(lines, BW),
+        table_id.reshape(lines, BW),
+        volume,
+        interp,
+    )
     target = target.reshape(block_count)
 
     hot = (groups[:, None] == jnp.arange(ctf.shape[0])[None, :]).astype(jnp.float32)
@@ -544,30 +605,38 @@
     gathered = gathered.reshape(slots, 2 * BW)
     cosine, sine = phases(shifts)
 
-    out_real, out_imag, evidence = pl.pallas_call(
+    keep, leave, evidence = pl.pallas_call(
         main_kernel,
         out_shape=(
-            jax.ShapeDtypeStruct((slots, BW), jnp.float32),
-            jax.ShapeDtypeStruct((slots, BW), jnp.float32),
+            jax.ShapeDtypeStruct((2, slots // 2, BW), jnp.float32),
+            jax.ShapeDtypeStruct((2, slots // 2, BW), jnp.bfloat16),
             jax.ShapeDtypeStruct((1, count), jnp.float32),
         ),
         in_specs=[pl.BlockSpec(memory_space=pltpu.SMEM)]
         + [pl.BlockSpec(memory_space=VMEM)] * 6,
-        out_specs=(pl.BlockSpec(memory_space=VMEM),) * 3,
+        out_specs=(
+            pl.BlockSpec(memory_space=pl.ANY),
+            pl.BlockSpec(memory_space=VMEM),
+            pl.BlockSpec(memory_space=VMEM),
+        ),
         scratch_shapes=[
             VMEM((slots, 2 * BW), jnp.float32),
-            VMEM((GROUP, R, BW), jnp.float32),
-            VMEM((GROUP, R, BW), jnp.float32),
+            VMEM((slots, BW), jnp.float32),
+            VMEM((slots, BW), jnp.float32),
+            VMEM((2 * GROUP, R, BW), jnp.float32),
+            VMEM((2 * GROUP, R, BW), jnp.float32),
             VMEM((R, KB * BW), jnp.float32),
+            VMEM((tries * R, GROUP * 2 * BW), jnp.bfloat16),
             VMEM((tries * R, GROUP * 2 * BW), jnp.bfloat16),
             VMEM((tries * R, count), jnp.float32),
             VMEM((tries * R, count), jnp.bfloat16),
+            pltpu.SemaphoreType.DMA((2,)),
         ],
         compiler_params=pltpu.CompilerParams(vmem_limit_bytes=48 << 20),
         name="score",
     )(target, gathered, weighted, hot, ctf, cosine, sine)
 
-    received_real, received_imag = collect(out_real, out_imag, devices, capacity)
+    received_real, received_imag = collect(keep, leave, devices, capacity)
     new_map = pl.pallas_call(
         end_kernel,
         out_shape=jax.ShapeDtypeStruct((blocks, 2 * BW), jnp.float32),

time: 133 us -> 118 us (0.89)
  Pallas kernels: 116 us -> 106 us
  other arithmetic: 5.82 us -> 3.54 us
  local copies, waits for them, and re-layouts: 9.47 us -> 7.38 us
    pallas_call x1, Pallas kernels: 41.2 us -> 32.3 us  [per_device(): pl.pallas_call(main_kernel, out_shape=(jax.ShapeDtypeStruct((2, slots //...]
    unnamed x20 -> x16, local copies, waits for them, and re-layouts: 9.39 us -> 7.38 us
    concatenate x1 -> x0, other arithmetic: 1.45 us -> none  [per_device(): jnp.concatenate(columns + [spare], axis=1)]
where the time goes in v4:
time: 118 us
  Pallas kernels  106 us (90%)
  local copies, waits for them, and re-layouts  7.38 us (6%)
  other arithmetic  3.54 us (3%)
    pallas_call x1, Pallas kernels, collect(): pl.pallas_call(functools.partial(collect_kernel, devices), out_shape=(jax...  35.3 us
    pallas_call x1, Pallas kernels, per_device(): pl.pallas_call(main_kernel, out_shape=(jax.ShapeDtypeStruct((2, slots //...  32.3 us
    pallas_call x1, Pallas kernels, spread(): pl.pallas_call(functools.partial(spread_kernel, devices), out_shape=(jax....  28.1 us
    unnamed x16, local copies, waits for them, and re-layouts  7.38 us
    pallas_call x1, Pallas kernels, per_device(): pl.pallas_call(functools.partial(prep_kernel, devices), out_shape=(jax.Sh...  6.32 us
    pallas_call x1, Pallas kernels, per_device(): pl.pallas_call(end_kernel, out_shape=jax.ShapeDtypeStruct((blocks, 2 * BW...  4.44 us

profile of v4, /device:TPU:0, one launch (start us, length us, event | category | flops | bytes accessed | tf_op | source)
XLA Modules:
  0.0 118.1 jit_solution(12729889449119196029)
XLA Ops:
  0.6 0.0 copy-start.3
  0.7 0.8 convert_bitcast_fusion.1
  1.4 0.1 broadcast_multiply_fusion.1
  1.5 0.1 broadcast_multiply_fusion
  1.6 0.7 fusion.2.hot_ref
  2.3 6.3 %prep.1 = (bf16[384,256]{1,0:T(8,128)(2,1)}, s32[32,128]{1,0:T(8,128)}, s32[1,384]{1,0:T(1,128)}, s32[384,1]{1,0:T(8,128)}) custom-call(s32[32,128]{1,0:T(8,128)} %bitcast.16, s32[32,128]{1,0:T(8,128)} %bitcast.17, s32[32,128]{1,0:T(8,128)} %bitcast.18, bf16[1024,256]{1,0:T(8,128)(2,1)} %volume_ref.3, bf16[8,128,128]{2,1,0:T(8,128)(2,1)} %interp_ref.3), custom_call_target="tpu_custom_call" | custom-call | tf_op jit(solution)/shard_map/prep/pallas_call | solution.py:585
  8.6 0.0 copy-start.7
  8.6 1.9 %fusion = (f32[64,9,128]{2,1,0:T(8,128)S(1)}, f32[64,9,128]{2,1,0:T(8,128)S(1)}) fusion(f32[64,9]{1,0:T(8,128)S(1)} %broadcast_multiply_fusion, f32[9,128]{1,0:T(8,128)S(1)} %broadcast_multiply_fusion.1), kind=kLoop, calls=%fused_computation.1 | loop fusion | flops 147456 | bytes 596736 | tf_op jit(solution)/shard_map/sin | solution.py:34
  10.5 0.0 copy-done.3
  10.5 0.0 copy-start.2
  10.6 1.6 %copy-done.2 = bf16[64,16384]{1,0:T(8,128)(2,1)S(1)} copy-done((bf16[64,16384]{1,0:T(8,128)(2,1)S(1)}, bf16[64,16384]{1,0:T(8,128)(2,1)}, u32[]{:S(2)}) %copy-start.2) | copy-done | bytes 2097176
  12.1 0.0 copy-start.4
  12.1 0.9 copy-done.4
  13.1 28.1 %spread.1 = (bf16[16,384,256]{2,1,0:T(8,128)(2,1)S(1)}, bf16[64,16384]{1,0:T(8,128)(2,1)S(1)}) custom-call(bf16[384,256]{1,0:T(8,128)(2,1)S(1)} %copy-done.4, bf16[64,16384]{1,0:T(8,128)(2,1)S(1)} %copy-done.2, f32[64,8]{1,0:T(8,128)S(1)} %fusion.2.hot_ref, f32[8,8192]{1,0:T(8,128)S(1)} %copy-done.3), custom_call_target="tpu_custom_call" | custom-call | tf_op jit(solution)/shard_map/spread/pallas_call | solution.py:524
  41.2 0.0 copy-start.1
  41.2 1.6 %copy-done.1 = bf16[16,384,256]{2,1,0:T(8,128)(2,1)} copy-done((bf16[16,384,256]{2,1,0:T(8,128)(2,1)}, bf16[16,384,256]{2,1,0:T(8,128)(2,1)S(1)}, u32[]{:S(2)}) %copy-start.1) | copy-done | bytes 3145752
  42.8 0.0 copy-done.7
  42.8 32.3 %score.1 = (f32[2,3072,128]{2,1,0:T(8,128)}, bf16[2,3072,128]{2,1,0:T(8,128)(2,1)S(1)}, f32[1,64]{1,0:T(1,128)}) custom-call(s32[4096]{0:T(1024)S(1)} %bitcast.15, bf16[6144,256]{1,0:T(8,128)(2,1)} %bitcast.13, bf16[64,16384]{1,0:T(8,128)(2,1)S(1)} %get-tuple-element.18.weighted_ref, f32[64,8]{1,0:T(8,128)S(1)} %fusion.2.hot_ref, f32[8,8192]{1,0:T(8,128)S(1)} %copy-done.3, ...), custom_call_target="tpu_custom_call" | custom-call | tf_op jit(solution)/shard_map/score/pallas_call | solution.py:608
  75.1 0.0 copy-start
  75.1 1.9 %copy-done = f32[2,3072,128]{2,1,0:T(8,128)S(1)} copy-done((f32[2,3072,128]{2,1,0:T(8,128)S(1)}, f32[2,3072,128]{2,1,0:T(8,128)}, u32[]{:S(2)}) %copy-start) | copy-done | bytes 3145752
  77.0 35.3 %collect.1 = (f32[384,128]{1,0:T(8,128)S(1)}, f32[384,128]{1,0:T(8,128)S(1)}) custom-call(f32[2,2,4,384,128]{4,3,2,1,0:T(8,128)S(1)} %bitcast.12, bf16[2,2,4,384,128]{4,3,2,1,0:T(8,128)(2,1)S(1)} %bitcast.14), custom_call_target="tpu_custom_call" | custom-call | tf_op jit(solution)/shard_map/collect/pallas_call | solution.py:550
  112.3 0.0 copy-start.5
  112.3 0.7 copy-done.5
  113.0 0.0 copy-start.6
  113.0 0.7 copy-done.6
  113.6 4.4 %finish.1 = f32[1024,256]{1,0:T(8,128)} custom-call(s32[1,384]{1,0:T(1,128)} %get-tuple-element.13.local_ref, s32[384,1]{1,0:T(8,128)} %get-tuple-element.14.table_ref, f32[384,128]{1,0:T(8,128)} %copy-done.5, f32[384,128]{1,0:T(8,128)} %copy-done.6, bf16[1024,256]{1,0:T(8,128)(2,1)} %volume_ref.3, bf16[8,128,128]{2,1,0:T(8,128)(2,1)} %interp_ref.3), custom_call_target="tpu_custom_call" | custom-call | tf_op jit(solution)/shard_map/finish/pallas_call | solution.py:640
  (2 shorter events, 0.0 us)
Async XLA Ops:
  0.6 9.9 %copy-start.3 = (f32[8,8192]{1,0:T(8,128)S(1)}, f32[8,8192]{1,0:T(8,128)}, u32[]{:S(2)}) copy-start(f32[8,8192]{1,0:T(8,128)} %ctf_ref.3) | copy-start | bytes 786436
  8.6 34.2 %copy-start.7 = (s32[32,128]{1,0:T(8,128)S(1)}, s32[32,128]{1,0:T(8,128)}, u32[]{:S(2)}) copy-start(s32[32,128]{1,0:T(8,128)} %get-tuple-element.15) | copy-start | bytes 49156
  10.5 1.6 %copy-start.2 = (bf16[64,16384]{1,0:T(8,128)(2,1)S(1)}, bf16[64,16384]{1,0:T(8,128)(2,1)}, u32[]{:S(2)}) copy-start(bf16[64,16384]{1,0:T(8,128)(2,1)} %images_ref.1) | copy-start | bytes 6291460
  12.1 0.9 copy-start.4
  41.2 1.6 %copy-start.1 = (bf16[16,384,256]{2,1,0:T(8,128)(2,1)}, bf16[16,384,256]{2,1,0:T(8,128)(2,1)S(1)}, u32[]{:S(2)}) copy-start(bf16[16,384,256]{2,1,0:T(8,128)(2,1)S(1)} %get-tuple-element.17) | copy-start | bytes 9437188
  75.1 1.9 %copy-start = (f32[2,3072,128]{2,1,0:T(8,128)S(1)}, f32[2,3072,128]{2,1,0:T(8,128)}, u32[]{:S(2)}) copy-start(f32[2,3072,128]{2,1,0:T(8,128)} %get-tuple-element.19) | copy-start | bytes 9437188
  112.3 0.7 copy-start.5
  113.0 0.7 copy-start.6

commit v5 on v4

--- a/solution.py
+++ b/solution.py
@@ -272,13 +272,15 @@
             out_real[row, :] = real_rows[k, r : r + 1, :]
             out_imag[row, :] = imag_rows[k, r : r + 1, :]
 
-    @pl.loop(0, KB // GROUP)
+    trip = 2 * GROUP
+
+    @pl.loop(0, KB // trip)
     def _(i):
-        for k in range(GROUP):
-            back(i * GROUP + k, k)
+        for k in range(trip):
+            back(i * trip + k, k)
             if k:
-                place(i * GROUP + k - 1, k - 1)
-        place(i * GROUP + GROUP - 1, GROUP - 1)
+                place(i * trip + k - 1, k - 1)
+        place(i * trip + trip - 1, trip - 1)
 
     half = slots // 2
     core = lax.axis_index("img") % 2
@@ -475,7 +477,7 @@
         aq = (a + da) % outer
         return own_box[db, part, aq] + core_box[db, part, aq].astype(jnp.float32)
 
-    steps = list(range(1, outer)) + [0]
+    steps = sorted(range(1, outer), key=lambda d: -min(d, outer - d)) + [0]
     for db in range(1, middle):
         for part in range(2):
             own[db, part].wait()

time: 118 us -> 117 us (level)
    pallas_call x1, Pallas kernels: 32.3 us -> 31 us  [per_device(): pl.pallas_call(main_kernel, out_shape=(jax.ShapeDtypeStruct((2, slots //...]
where the time goes in v5:
time: 117 us; the launch traced here: 116 us
  Pallas kernels  105 us (90%)
  local copies, waits for them, and re-layouts  7.38 us (6%)
  other arithmetic  3.54 us (3%)
    pallas_call x1, Pallas kernels, collect(): pl.pallas_call(functools.partial(collect_kernel, devices), out_shape=(jax...  34.7 us
    pallas_call x1, Pallas kernels, per_device(): pl.pallas_call(main_kernel, out_shape=(jax.ShapeDtypeStruct((2, slots //...  31 us
    pallas_call x1, Pallas kernels, spread(): pl.pallas_call(functools.partial(spread_kernel, devices), out_shape=(jax....  28.1 us
    unnamed x16, local copies, waits for them, and re-layouts  7.38 us
    pallas_call x1, Pallas kernels, per_device(): pl.pallas_call(functools.partial(prep_kernel, devices), out_shape=(jax.Sh...  6.32 us
    pallas_call x1, Pallas kernels, per_device(): pl.pallas_call(end_kernel, out_shape=jax.ShapeDtypeStruct((blocks, 2 * BW...  4.44 us

profile of v5, /device:TPU:0, one launch (start us, length us, event | category | flops | bytes accessed | tf_op | source)
XLA Modules:
  0.0 116.3 jit_solution(5173222293846146764)
XLA Ops:
  0.6 0.0 copy-start.3
  0.7 0.8 convert_bitcast_fusion.1
  1.4 0.1 broadcast_multiply_fusion.1
  1.5 0.1 broadcast_multiply_fusion
  1.6 0.7 fusion.2.hot_ref
  2.3 6.3 %prep.1 = (bf16[384,256]{1,0:T(8,128)(2,1)}, s32[32,128]{1,0:T(8,128)}, s32[1,384]{1,0:T(1,128)}, s32[384,1]{1,0:T(8,128)}) custom-call(s32[32,128]{1,0:T(8,128)} %bitcast.16, s32[32,128]{1,0:T(8,128)} %bitcast.17, s32[32,128]{1,0:T(8,128)} %bitcast.18, bf16[1024,256]{1,0:T(8,128)(2,1)} %volume_ref.3, bf16[8,128,128]{2,1,0:T(8,128)(2,1)} %interp_ref.3), custom_call_target="tpu_custom_call" | custom-call | tf_op jit(solution)/shard_map/prep/pallas_call | solution.py:587
  8.6 0.0 copy-start.7
  8.6 1.9 %fusion = (f32[64,9,128]{2,1,0:T(8,128)S(1)}, f32[64,9,128]{2,1,0:T(8,128)S(1)}) fusion(f32[64,9]{1,0:T(8,128)S(1)} %broadcast_multiply_fusion, f32[9,128]{1,0:T(8,128)S(1)} %broadcast_multiply_fusion.1), kind=kLoop, calls=%fused_computation.1 | loop fusion | flops 147456 | bytes 596736 | tf_op jit(solution)/shard_map/sin | solution.py:34
  10.5 0.0 copy-done.3
  10.5 0.0 copy-start.2
  10.6 1.6 %copy-done.2 = bf16[64,16384]{1,0:T(8,128)(2,1)S(1)} copy-done((bf16[64,16384]{1,0:T(8,128)(2,1)S(1)}, bf16[64,16384]{1,0:T(8,128)(2,1)}, u32[]{:S(2)}) %copy-start.2) | copy-done | bytes 2097176
  12.1 0.0 copy-start.4
  12.1 0.9 copy-done.4
  13.1 28.1 %spread.1 = (bf16[16,384,256]{2,1,0:T(8,128)(2,1)S(1)}, bf16[64,16384]{1,0:T(8,128)(2,1)S(1)}) custom-call(bf16[384,256]{1,0:T(8,128)(2,1)S(1)} %copy-done.4, bf16[64,16384]{1,0:T(8,128)(2,1)S(1)} %copy-done.2, f32[64,8]{1,0:T(8,128)S(1)} %fusion.2.hot_ref, f32[8,8192]{1,0:T(8,128)S(1)} %copy-done.3), custom_call_target="tpu_custom_call" | custom-call | tf_op jit(solution)/shard_map/spread/pallas_call | solution.py:526
  41.2 0.0 copy-start.1
  41.2 1.6 %copy-done.1 = bf16[16,384,256]{2,1,0:T(8,128)(2,1)} copy-done((bf16[16,384,256]{2,1,0:T(8,128)(2,1)}, bf16[16,384,256]{2,1,0:T(8,128)(2,1)S(1)}, u32[]{:S(2)}) %copy-start.1) | copy-done | bytes 3145752
  42.8 0.0 copy-done.7
  42.8 31.0 %score.1 = (f32[2,3072,128]{2,1,0:T(8,128)}, bf16[2,3072,128]{2,1,0:T(8,128)(2,1)S(1)}, f32[1,64]{1,0:T(1,128)}) custom-call(s32[4096]{0:T(1024)S(1)} %bitcast.15, bf16[6144,256]{1,0:T(8,128)(2,1)} %bitcast.13, bf16[64,16384]{1,0:T(8,128)(2,1)S(1)} %get-tuple-element.18.weighted_ref, f32[64,8]{1,0:T(8,128)S(1)} %fusion.2.hot_ref, f32[8,8192]{1,0:T(8,128)S(1)} %copy-done.3, ...), custom_call_target="tpu_custom_call" | custom-call | tf_op jit(solution)/shard_map/score/pallas_call | solution.py:610
  73.9 0.0 copy-start
  73.9 1.9 %copy-done = f32[2,3072,128]{2,1,0:T(8,128)S(1)} copy-done((f32[2,3072,128]{2,1,0:T(8,128)S(1)}, f32[2,3072,128]{2,1,0:T(8,128)}, u32[]{:S(2)}) %copy-start) | copy-done | bytes 3145752
  75.8 34.7 %collect.1 = (f32[384,128]{1,0:T(8,128)S(1)}, f32[384,128]{1,0:T(8,128)S(1)}) custom-call(f32[2,2,4,384,128]{4,3,2,1,0:T(8,128)S(1)} %bitcast.12, bf16[2,2,4,384,128]{4,3,2,1,0:T(8,128)(2,1)S(1)} %bitcast.14), custom_call_target="tpu_custom_call" | custom-call | tf_op jit(solution)/shard_map/collect/pallas_call | solution.py:552
  110.5 0.0 copy-start.5
  110.5 0.7 copy-done.5
  111.2 0.0 copy-start.6
  111.2 0.7 copy-done.6
  111.9 4.4 %finish.1 = f32[1024,256]{1,0:T(8,128)} custom-call(s32[1,384]{1,0:T(1,128)} %get-tuple-element.13.local_ref, s32[384,1]{1,0:T(8,128)} %get-tuple-element.14.table_ref, f32[384,128]{1,0:T(8,128)} %copy-done.5, f32[384,128]{1,0:T(8,128)} %copy-done.6, bf16[1024,256]{1,0:T(8,128)(2,1)} %volume_ref.3, bf16[8,128,128]{2,1,0:T(8,128)(2,1)} %interp_ref.3), custom_call_target="tpu_custom_call" | custom-call | tf_op jit(solution)/shard_map/finish/pallas_call | solution.py:642
  (2 shorter events, 0.0 us)
Async XLA Ops:
  0.6 9.9 %copy-start.3 = (f32[8,8192]{1,0:T(8,128)S(1)}, f32[8,8192]{1,0:T(8,128)}, u32[]{:S(2)}) copy-start(f32[8,8192]{1,0:T(8,128)} %ctf_ref.3) | copy-start | bytes 786436
  8.6 34.2 %copy-start.7 = (s32[32,128]{1,0:T(8,128)S(1)}, s32[32,128]{1,0:T(8,128)}, u32[]{:S(2)}) copy-start(s32[32,128]{1,0:T(8,128)} %get-tuple-element.15) | copy-start | bytes 49156
  10.5 1.6 %copy-start.2 = (bf16[64,16384]{1,0:T(8,128)(2,1)S(1)}, bf16[64,16384]{1,0:T(8,128)(2,1)}, u32[]{:S(2)}) copy-start(bf16[64,16384]{1,0:T(8,128)(2,1)} %images_ref.1) | copy-start | bytes 6291460
  12.1 0.9 copy-start.4
  41.2 1.6 %copy-start.1 = (bf16[16,384,256]{2,1,0:T(8,128)(2,1)}, bf16[16,384,256]{2,1,0:T(8,128)(2,1)S(1)}, u32[]{:S(2)}) copy-start(bf16[16,384,256]{2,1,0:T(8,128)(2,1)S(1)} %get-tuple-element.17) | copy-start | bytes 9437188
  73.9 1.9 %copy-start = (f32[2,3072,128]{2,1,0:T(8,128)S(1)}, f32[2,3072,128]{2,1,0:T(8,128)}, u32[]{:S(2)}) copy-start(f32[2,3072,128]{2,1,0:T(8,128)} %get-tuple-element.19) | copy-start | bytes 9437188
  110.5 0.7 copy-start.5
  111.2 0.7 copy-start.6
